TPU v7x, 32 devices: a whole 2x2x4 slice. The times are simulated.
32 devices in a mesh: groups: 2 (over y), seq: 4 (over z), pool: 2 (over x), branch: 2 (over core).
Axes of the slice: x: 2, y: 2, z: 4, core: 2. Of those that a mesh axis runs over, the one named last changes fastest.
Arguments:
- video_query: bfloat16 [2, 4096, 3072], P('branch', ('groups', 'seq'), 'pool'), parts along dimension 1, may hold values from -6 to 6
- video_key: bfloat16 [2, 4096, 3072], P('branch', ('groups', 'seq'), 'pool'), parts along dimension 1, may hold values from -6 to 6
- video_value: bfloat16 [2, 4096, 3072], P('branch', ('groups', 'seq'), 'pool'), parts along dimension 1, may hold values from -6 to 6
- cross_query: bfloat16 [2, 4096, 3072], P('branch', ('groups', 'seq'), 'pool'), parts along dimension 1, may hold values from -6 to 6
- audio_key: bfloat16 [2, 512, 3072], P('branch', ('groups', 'seq'), 'pool'), parts along dimension 1, may hold values from -6 to 6
- audio_value: bfloat16 [2, 512, 3072], P('branch', ('groups', 'seq'), 'pool'), parts along dimension 1, may hold values from -6 to 6
- tile_list: int32 [32, 3], P(('groups', 'seq')), parts along dimension 0, may hold values from 0 to 3, as said below
- tile_count: int32 [32], P(('groups', 'seq')), parts along dimension 0, may hold values from 1 to 3
Outputs:
- guided_self: bfloat16 [4096, 3072], P(('groups', 'seq', 'branch'), 'pool'), parts along dimension 0
- guided_cross: bfloat16 [4096, 3072], P(('groups', 'seq', 'branch'), 'pool'), parts along dimension 0
There are 2 independent parts, one for each index of `groups`. A program takes and returns all parts, laid end to end along the dimension named above; each array names one. Nothing has to cross between parts.
Inputs may be any that keep to these rules, and one draw needn't show every extreme that they name: `tile_list`: entry 0 of row v is a = v // 4, the audio tile aligned with video tile v; entries 1 and 2 are a - 1 and a + 1 in an order drawn per row, each clipped to the existing tiles.
All inputs are finite; a program needn't handle non-finite values.
Results may differ from a plain program's by a relative error of at most 0.0051.
Values may be sent and summed in bfloat16 or wider, within the bound.
No kernel may reach another device: no remote copies, remote signals or barrier semaphores. Data moves between devices by JAX's collectives and lax.ppermute only.
A program may use at most 64 MiB of HBM per device.

v0:
```python
import math

import jax
import jax.numpy as jnp
from jax import lax
from jax.experimental import pallas as pl
from jax.experimental.pallas import tpu as pltpu
from jax.sharding import PartitionSpec as P


DH = 128
VTILE = 128
ATILE = 64
KMAX = 3

guidance_weight = 4.0
far_below = -1e30
exp2_scale = DH**-0.5 * math.log2(math.e)


def shifted(block, axis, distance):
    count = lax.axis_size(axis)
    return lax.ppermute(block, axis, [(i, (i + distance) % count) for i in range(count)])


def neighbour(block, axis, step):
    count = lax.axis_size(axis)
    route = [(i, i + step) for i in range(count) if 0 <= i + step < count]
    return lax.ppermute(block, axis, route)


def transposed_dot(left, right):
    return lax.dot_general(left, right, (((1,), (1,)), ((), ())), preferred_element_type=jnp.float32)


def pack(where, tensors, head, heads_dest, count):
    rows = tensors[0].shape[1]
    kinds = len(tensors)

    def kernel(where_ref, *refs):
        ins, outs = refs[: kinds * (count - 1)], refs[kinds * (count - 1) :]
        for k in range(count - 1):
            for t in range(kinds):
                outs[k][t] = ins[kinds * k + t][0]

    def column(k):
        return lambda i, w: (0, 0, ((w[0] + k) % count) * heads_dest + head)

    return pl.pallas_call(
        kernel,
        grid_spec=pltpu.PrefetchScalarGridSpec(
            num_scalar_prefetch=1,
            grid=(1,),
            in_specs=[
                pl.BlockSpec((1, rows, DH), column(k))
                for k in range(1, count)
                for _ in range(kinds)
            ],
            out_specs=[pl.BlockSpec((kinds, rows, DH), lambda i, w: (0, 0, 0))] * (count - 1),
        ),
        out_shape=[jax.ShapeDtypeStruct((kinds, rows, DH), jnp.bfloat16)] * (count - 1),
        cost_estimate=pl.CostEstimate(
            flops=0, bytes_accessed=2 * kinds * (count - 1) * rows * DH * 2, transcendentals=0
        ),
        name="pack",
    )(where, *(tuple(tensors) * (count - 1)))


def attend(where, tensors, queries, pairs, head, heads_dest):
    rows = tensors[0].shape[1]
    count = len(pairs) + 1
    half = rows // 2
    shared = queries is pairs
    operands = [*tensors, *pairs] + ([] if shared else queries)

    def kernel(where_ref, q_ref, k_ref, v_ref, *refs):
        pair_refs, refs = refs[: count - 1], refs[count - 1 :]
        query_refs = pair_refs if shared else refs[: count - 1]
        keep_ref, send_ref, qs, ks, vs, sems = refs[-6:]
        column = pl.ds(pl.multiple_of((where_ref[0] * heads_dest + head) * DH, DH), DH)

        def fetch(r, own, other, at, scratch, sem):
            source = other[r - 1].at[at] if r else own.at[0, :, column]
            return pltpu.make_async_copy(source, scratch.at[r * rows : (r + 1) * rows], sem)

        key_copies = [
            fetch(r, k_ref, pair_refs, pairs[0].shape[0] - 2, ks, sems.at[0, r])
            for r in range(count)
        ]
        query_copies = [
            fetch(r, q_ref, query_refs, 0, qs, sems.at[1, r]) for r in range(count)
        ]
        value_copies = [
            fetch(r, v_ref, pair_refs, pairs[0].shape[0] - 1, vs, sems.at[2, r])
            for r in range(count)
        ]
        for copy in key_copies + query_copies + value_copies:
            copy.start()
        for copy in key_copies + query_copies + value_copies:
            copy.wait()
        copy_index = where_ref[1]

        def part(start):
            q = qs[pl.ds(pl.multiple_of(start, half), half), :]
            scores = transposed_dot(q, ks[...])
            highest = jnp.max(scores, axis=1, keepdims=True)
            expo = jnp.exp2((scores - highest) * exp2_scale)
            denom = jnp.sum(expo, axis=1, keepdims=True)
            numer = jnp.dot(expo.astype(jnp.bfloat16), vs[...], preferred_element_type=jnp.float32)
            return (numer / denom).astype(jnp.bfloat16)

        @pl.loop(0, count)
        def _(i):
            keep_ref[i] = part(i * rows + copy_index * half)
            send_ref[i] = part(i * rows + (1 - copy_index) * half)

    tokens = count * rows
    out = pl.BlockSpec((count, half, DH), lambda i, w: (0, 0, 0))
    return pl.pallas_call(
        kernel,
        grid_spec=pltpu.PrefetchScalarGridSpec(
            num_scalar_prefetch=1,
            grid=(1,),
            in_specs=[pl.BlockSpec(memory_space=pl.ANY)] * len(operands),
            out_specs=[out, out],
            scratch_shapes=[pltpu.VMEM((tokens, DH), jnp.bfloat16)] * 3
            + [pltpu.SemaphoreType.DMA((3, count))],
        ),
        out_shape=[jax.ShapeDtypeStruct((count, half, DH), jnp.bfloat16)] * 2,
        cost_estimate=pl.CostEstimate(
            flops=4 * tokens * tokens * DH,
            bytes_accessed=4 * tokens * DH * 2,
            transcendentals=tokens * tokens,
        ),
        name="attend",
    )(where, *operands)


def combine(where, keep, other):
    here, half, width = keep.shape

    def kernel(where_ref, keep_ref, other_ref, *outs):
        first = where_ref[1] == 0
        for i in range(here):
            mine = keep_ref[i].astype(jnp.float32)
            theirs = other_ref[i].astype(jnp.float32)
            cond = jnp.where(first, mine, theirs)
            uncond = jnp.where(first, theirs, mine)
            outs[i][...] = (uncond + guidance_weight * (cond - uncond)).astype(jnp.bfloat16)

    whole = pl.BlockSpec((here, half, width), lambda i, w: (0, 0, 0))
    return pl.pallas_call(
        kernel,
        grid_spec=pltpu.PrefetchScalarGridSpec(
            num_scalar_prefetch=1,
            grid=(1,),
            in_specs=[whole, whole],
            out_specs=[pl.BlockSpec((half, width), lambda i, w: (0, 0))] * here,
        ),
        out_shape=[jax.ShapeDtypeStruct((half, width), jnp.bfloat16)] * here,
        cost_estimate=pl.CostEstimate(
            flops=0, bytes_accessed=3 * here * half * width * 2, transcendentals=0
        ),
        name="combine",
    )(where, keep, other)


def column_of(where_ref, head, r, heads_dest, count):
    column = (lax.rem(where_ref[0] + r, count) * heads_dest + head) * DH
    return pl.ds(pl.multiple_of(column, DH), DH)


def assemble(where, pieces, heads_dest, count):
    places = list(pieces)
    half = pieces[places[0]].shape[0]

    def kernel(where_ref, *refs):
        ins, out = refs[:-1], refs[-1]
        for place, ref in zip(places, ins):
            out[:, column_of(where_ref, *place, heads_dest, count)] = ref[...]

    block = pl.BlockSpec((half, DH), lambda i, w: (0, 0))
    width = heads_dest * count * DH
    return pl.pallas_call(
        kernel,
        grid_spec=pltpu.PrefetchScalarGridSpec(
            num_scalar_prefetch=1,
            grid=(1,),
            in_specs=[block] * len(places),
            out_specs=pl.BlockSpec((half, width), lambda i, w: (0, 0)),
        ),
        out_shape=jax.ShapeDtypeStruct((half, width), jnp.bfloat16),
        cost_estimate=pl.CostEstimate(
            flops=0, bytes_accessed=2 * half * width * 2, transcendentals=0
        ),
        name="assemble",
    )(where, *pieces.values())


def complete(where, partial, pieces, heads_dest, count):
    places = list(pieces)
    half, width = partial.shape

    def kernel(where_ref, partial_ref, *refs):
        ins, out, sems = refs[:-2], refs[-2], refs[-1]
        copies = [
            pltpu.make_async_copy(
                ref, out.at[:, column_of(where_ref, *place, heads_dest, count)], sems.at[i]
            )
            for i, (place, ref) in enumerate(zip(places, ins))
        ]
        for copy in copies:
            copy.start()
        for copy in copies:
            copy.wait()

    return pl.pallas_call(
        kernel,
        grid_spec=pltpu.PrefetchScalarGridSpec(
            num_scalar_prefetch=1,
            grid=(1,),
            in_specs=[pl.BlockSpec(memory_space=pl.ANY)]
            + [pl.BlockSpec((half, DH), lambda i, w: (0, 0))] * len(places),
            out_specs=pl.BlockSpec(memory_space=pl.ANY),
            scratch_shapes=[pltpu.SemaphoreType.DMA((len(places),))],
        ),
        out_shape=jax.ShapeDtypeStruct((half, width), jnp.bfloat16),
        input_output_aliases={1: 0},
        cost_estimate=pl.CostEstimate(
            flops=0, bytes_accessed=2 * half * DH * len(places) * 2, transcendentals=0
        ),
        name="complete",
    )(where, partial, *pieces.values())


def send_order(count):
    return sorted(range(1, count), key=lambda k: -min(k, count - k))


def self_by_heads(where, video_query, video_key, video_value):
    count = lax.axis_size("seq")
    heads_dest = video_query.shape[2] // DH // count
    tensors = (video_query, video_key, video_value)
    order = send_order(count)
    last = heads_dest - 1

    def inflow(kinds, head):
        sent = pack(where, kinds, head, heads_dest, count)
        received = [None] * (count - 1)
        for k in order:
            received[k - 1] = shifted(sent[k - 1], "seq", k)
        return received

    def outflow(queries, pairs, head):
        keep, send = attend(where, tensors, queries, pairs, head, heads_dest)
        other = shifted(send, "branch", 1)
        guided = combine(where, keep, other)
        done = {(head, 0): guided[0]}
        for r in order:
            done[head, r] = shifted(guided[r], "seq", -r)
        return done

    received = [inflow(tensors, head) for head in range(heads_dest)]
    pieces = {}
    for head in range(last):
        pieces |= outflow(received[head], received[head], head)
    final = outflow(received[last], received[last], last)
    pieces[last, 0] = final.pop((last, 0))
    partial = assemble(where, pieces, heads_dest, count)
    return complete(where, partial, final, heads_dest, count)


def self_by_rows(video_query, video_key, video_value):
    rows = video_query.shape[1]
    width = video_query.shape[2]
    heads_dev = width // DH
    scale = DH ** (-0.5)
    queries = video_query[0].reshape(rows, heads_dev, DH)
    start_max = jnp.full((heads_dev, rows), far_below, jnp.float32)
    start_total = jnp.zeros((heads_dev, rows), jnp.float32)
    start_accum = jnp.zeros((heads_dev, rows, DH), jnp.float32)
    key_piece = lax.all_gather(video_key[0], "seq", axis=0, tiled=True)
    value_piece = lax.all_gather(video_value[0], "seq", axis=0, tiled=True)
    count = key_piece.shape[0]
    block = math.gcd(count, 512)
    steps = count // block
    key_blocks = key_piece.reshape(steps, block, heads_dev, DH)
    value_blocks = value_piece.reshape(steps, block, heads_dev, DH)

    def one_block(state, pair):
        running_max, total, accum = state
        key_block, value_block = pair
        scores = (
            jnp.einsum("qhd,khd->hqk", queries, key_block, preferred_element_type=jnp.float32)
            * scale
        )
        new_max = jnp.maximum(running_max, jnp.max(scores, axis=-1))
        factor = jnp.exp(running_max - new_max)
        expo = jnp.exp(scores - new_max[:, :, None])
        total = total * factor + jnp.sum(expo, axis=-1)
        accum = accum * factor[:, :, None] + jnp.einsum(
            "hqk,khd->hqd",
            expo.astype(jnp.bfloat16),
            value_block,
            preferred_element_type=jnp.float32,
        )
        return ((new_max, total, accum), None)

    state, _ = lax.scan(
        one_block, (start_max, start_total, start_accum), (key_blocks, value_blocks)
    )
    _, total, accum = state
    result = (accum / total[:, :, None]).astype(jnp.bfloat16)
    heads = jnp.transpose(result, (1, 0, 2)).reshape(rows, width)
    half = rows // 2
    copy_index = lax.axis_index("branch")
    keep = lax.dynamic_slice_in_dim(heads, copy_index * half, half, 0)
    send = lax.dynamic_slice_in_dim(heads, (1 - copy_index) * half, half, 0)
    return guide(keep, shifted(send, "branch", 1))


def guide(keep, other):
    is_first = lax.axis_index("branch") == 0
    cond = jnp.where(is_first, keep, other).astype(jnp.float32)
    uncond = jnp.where(is_first, other, keep).astype(jnp.float32)
    return (uncond + guidance_weight * (cond - uncond)).astype(jnp.bfloat16)


def cross(where, cross_query, audio_key, audio_value, tile_list, tile_count):
    rows = cross_query.shape[1]
    width = cross_query.shape[2]
    half = rows // 2
    tiles = rows // VTILE
    keys_here = 3 * ATILE
    heads_step = math.gcd(width // DH, 3)
    block = heads_step * DH
    sides = [(neighbour(a, "seq", 1), a, neighbour(a, "seq", -1)) for a in (audio_key, audio_value)]
    tile_ids = where[0] - 1 + jnp.arange(keys_here, dtype=jnp.int32) // ATILE
    live = jnp.arange(KMAX, dtype=jnp.int32)[None, :] < tile_count[:, None]
    allowed = jnp.any(live[:, :, None] & (tile_list[:, :, None] == tile_ids[None, None, :]), axis=1)

    def kernel(where_ref, allowed_ref, q_ref, *refs):
        key_refs, value_refs = refs[:3], refs[3:6]
        keep_ref, send_ref, result = refs[6:]
        mask = jnp.concatenate(
            [
                jnp.broadcast_to(allowed_ref[v : v + 1, :] != 0, (VTILE, keys_here))
                for v in range(tiles)
            ],
            axis=0,
        )
        for h in range(heads_step):
            at = slice(h * DH, (h + 1) * DH)
            keys = jnp.concatenate([ref[0, :, at] for ref in key_refs], axis=0)
            values = jnp.concatenate([ref[0, :, at] for ref in value_refs], axis=0)
            scores = jnp.where(mask, transposed_dot(q_ref[0, :, at], keys), far_below)
            highest = jnp.max(scores, axis=1, keepdims=True)
            expo = jnp.exp2((scores - highest) * exp2_scale)
            denom = jnp.sum(expo, axis=1, keepdims=True)
            numer = jnp.dot(expo.astype(jnp.bfloat16), values, preferred_element_type=jnp.float32)
            result[:, at] = (numer / denom).astype(jnp.bfloat16)
        for ref, which in ((keep_ref, where_ref[1]), (send_ref, 1 - where_ref[1])):
            ref[...] = result[pl.ds(pl.multiple_of(which * half, half), half), :]

    audio = pl.BlockSpec((1, ATILE, block), lambda h, w: (0, 0, h))
    out = pl.BlockSpec((half, block), lambda h, w: (0, h))
    call = pl.pallas_call(
        kernel,
        grid_spec=pltpu.PrefetchScalarGridSpec(
            num_scalar_prefetch=1,
            grid=(width // block,),
            in_specs=[
                pl.BlockSpec((tiles, keys_here), lambda h, w: (0, 0)),
                pl.BlockSpec((1, rows, block), lambda h, w: (0, 0, h)),
                *[audio] * 6,
            ],
            out_specs=[out, out],
            scratch_shapes=[pltpu.VMEM((rows, block), jnp.bfloat16)],
        ),
        out_shape=[jax.ShapeDtypeStruct((half, width), jnp.bfloat16)] * 2,
        cost_estimate=pl.CostEstimate(
            flops=4 * rows * width * keys_here,
            bytes_accessed=2 * rows * width * 2,
            transcendentals=rows * (width // DH) * keys_here,
        ),
        name="cross_kernel",
    )
    keep, send = call(where, allowed.astype(jnp.int32), cross_query, *sides[0], *sides[1])
    other = shifted(send, "branch", 1)
    return guide(keep, other)


def shards(
    video_query, video_key, video_value, cross_query, audio_key, audio_value, tile_list, tile_count
):
    where = jnp.stack([lax.axis_index("seq"), lax.axis_index("branch")]).astype(jnp.int32)
    heads_dev = video_query.shape[2] // DH
    guided_cross = cross(where, cross_query, audio_key, audio_value, tile_list, tile_count)
    if heads_dev % lax.axis_size("seq") == 0:
        guided_self = self_by_heads(where, video_query, video_key, video_value)
    else:
        guided_self = self_by_rows(video_query, video_key, video_value)
    return (guided_self, guided_cross)


def solution(mesh):
    placed = (
        P("branch", ("groups", "seq"), "pool"),
        P("branch", ("groups", "seq"), "pool"),
        P("branch", ("groups", "seq"), "pool"),
        P("branch", ("groups", "seq"), "pool"),
        P("branch", ("groups", "seq"), "pool"),
        P("branch", ("groups", "seq"), "pool"),
        P(("groups", "seq"), None),
        P(("groups", "seq")),
    )
    return jax.shard_map(
        shards,
        mesh=mesh,
        in_specs=placed,
        out_specs=(P(("groups", "seq", "branch"), "pool"), P(("groups", "seq", "branch"), "pool")),
        check_vma=False,
    )
```

profile of v0, /device:TPU:0, one launch (start us, length us, event | category | flops | bytes accessed | tf_op | source)
XLA Modules:
  0.0 165.1 jit_solution(4580294322427278883)
XLA Ops:
  0.6 5.0 %collective-permute-start.21 = (bf16[1,64,1536]{2,1,0:T(8,128)(2,1)}, bf16[1,64,1536]{2,1,0:T(8,128)(2,1)S(1)}, u32[]{:S(2)}, u32[]{:S(2)}) collective-permute-start(bf16[1,64,1536]{2,1,0:T(8,128)(2,1)} %refs_1_.7), channel_id=1, source_target_pairs={{0,4},{4,8},{8,12},{1,5},{5,9},{9,13},{2,6},{6,10},{10,14},{3,7},{... | collective-permute-start | bytes 589832 | tf_op jit(solution)/shard_map/ppermute | solution.py:29
  5.6 1.3 collective-permute-start.22
  6.9 4.6 %collective-permute-start.23 = (bf16[1,64,1536]{2,1,0:T(8,128)(2,1)}, bf16[1,64,1536]{2,1,0:T(8,128)(2,1)S(1)}, u32[]{:S(2)}, u32[]{:S(2)}) collective-permute-start(bf16[1,64,1536]{2,1,0:T(8,128)(2,1)} %refs_4_.7), channel_id=1, source_target_pairs={{0,4},{4,8},{8,12},{1,5},{5,9},{9,13},{2,6},{6,10},{10,14},{3,7},{... | collective-permute-start | bytes 589832 | tf_op jit(solution)/shard_map/ppermute | solution.py:29
  12.1 3.2 %pack.4 = (bf16[3,512,128]{2,1,0:T(8,128)(2,1)}, bf16[3,512,128]{2,1,0:T(8,128)(2,1)}, bf16[3,512,128]{2,1,0:T(8,128)(2,1)}) custom-call(s32[2]{0:T(128)} %pad_add_fusion.where_ref, bf16[1,512,1536]{2,1,0:T(8,128)(2,1)} %q_ref.6, bf16[1,512,1536]{2,1,0:T(8,128)(2,1)} %k_ref.5, bf16[1,512,1536]{2,1,0:T(8,128)(2,1)} %v_ref.5, bf16[1,512,1536]{2,1,0:T(8,128)(2,1)} %q_ref.6, ...), custom_call_target="tpu_custom_call" | custom-call | bytes 2359296 | tf_op jit(solution)/shard_map/pack/pallas_call | solution.py:49
  15.3 1.6 collective-permute-start.7
  18.2 3.1 %pack.3 = (bf16[3,512,128]{2,1,0:T(8,128)(2,1)}, bf16[3,512,128]{2,1,0:T(8,128)(2,1)}, bf16[3,512,128]{2,1,0:T(8,128)(2,1)}) custom-call(s32[2]{0:T(128)} %pad_add_fusion.where_ref, bf16[1,512,1536]{2,1,0:T(8,128)(2,1)} %q_ref.6, bf16[1,512,1536]{2,1,0:T(8,128)(2,1)} %k_ref.5, bf16[1,512,1536]{2,1,0:T(8,128)(2,1)} %v_ref.5, bf16[1,512,1536]{2,1,0:T(8,128)(2,1)} %q_ref.6, ...), custom_call_target="tpu_custom_call" | custom-call | bytes 2359296 | tf_op jit(solution)/shard_map/pack/pallas_call | solution.py:49
  21.3 3.7 %collective-permute-start.8 = (bf16[3,512,128]{2,1,0:T(8,128)(2,1)}, bf16[3,512,128]{2,1,0:T(8,128)(2,1)S(1)}, u32[]{:S(2)}, u32[]{:S(2)}) collective-permute-start(bf16[3,512,128]{2,1,0:T(8,128)(2,1)} %get-tuple-element.41), channel_id=1, source_target_pairs={{0,8},{4,12},{8,0},{12,4},{1,9},{5,13},{9,1},{13,5},{2,10},{6,14},... | collective-permute-start | bytes 1179656 | tf_op jit(solution)/shard_map/ppermute | solution.py:23
  25.0 1.4 collective-permute-start.9
  27.1 4.5 %collective-permute-done.24.refs_5_ = bf16[1,64,1536]{2,1,0:T(8,128)(2,1)S(1)} collective-permute-done((bf16[1,64,1536]{2,1,0:T(8,128)(2,1)S(1)}, bf16[1,64,1536]{2,1,0:T(8,128)(2,1)S(1)}, u32[]{:S(2)}, u32[]{:S(2)}) %collective-permute-start.24) | collective-permute-done | bytes 196640 | tf_op jit(solution)/shard_map/ppermute | solution.py:29
  31.6 2.5 %collective-permute-start.1 = (bf16[3,512,128]{2,1,0:T(8,128)(2,1)}, bf16[3,512,128]{2,1,0:T(8,128)(2,1)}, u32[]{:S(2)}, u32[]{:S(2)}) collective-permute-start(bf16[3,512,128]{2,1,0:T(8,128)(2,1)} %get-tuple-element.32), channel_id=1, source_target_pairs={{0,8},{4,12},{8,0},{12,4},{1,9},{5,13},{9,1},{13,5},{2,10},{6,14},... | collective-permute-start | bytes 1179656 | tf_op jit(solution)/shard_map/ppermute | solution.py:23
  34.1 6.9 %collective-permute-start.2 = (bf16[3,512,128]{2,1,0:T(8,128)(2,1)}, bf16[3,512,128]{2,1,0:T(8,128)(2,1)}, u32[]{:S(2)}, u32[]{:S(2)}) collective-permute-start(bf16[3,512,128]{2,1,0:T(8,128)(2,1)} %get-tuple-element.33), channel_id=1, source_target_pairs={{0,12},{4,0},{8,4},{12,8},{1,13},{5,1},{9,5},{13,9},{2,14},{6,2},{... | collective-permute-start | bytes 1179656 | tf_op jit(solution)/shard_map/ppermute | solution.py:23
  41.1 3.2 %pack.5 = (bf16[3,512,128]{2,1,0:T(8,128)(2,1)}, bf16[3,512,128]{2,1,0:T(8,128)(2,1)}, bf16[3,512,128]{2,1,0:T(8,128)(2,1)}) custom-call(s32[2]{0:T(128)} %pad_add_fusion.where_ref, bf16[1,512,1536]{2,1,0:T(8,128)(2,1)} %q_ref.6, bf16[1,512,1536]{2,1,0:T(8,128)(2,1)} %k_ref.5, bf16[1,512,1536]{2,1,0:T(8,128)(2,1)} %v_ref.5, bf16[1,512,1536]{2,1,0:T(8,128)(2,1)} %q_ref.6, ...), custom_call_target="tpu_custom_call" | custom-call | bytes 2359296 | tf_op jit(solution)/shard_map/pack/pallas_call | solution.py:49
  45.1 6.9 %cross_kernel.1 = (bf16[256,1536]{1,0:T(8,128)(2,1)}, bf16[256,1536]{1,0:T(8,128)(2,1)}) custom-call(s32[2]{0:T(128)} %pad_add_fusion.where_ref, s32[4,192]{1,0:T(4,128)} %convert_element_type.12.allowed_ref, bf16[1,512,1536]{2,1,0:T(8,128)(2,1)} %q_ref.7, bf16[1,64,1536]{2,1,0:T(8,128)(2,1)} %copy-done.5, bf16[1,64,1536]{2,1,0:T(8,128)(2,1)} %refs_1_.7, ...), custom_call_target="tpu_custom_call" | custom-call | flops 603979776 | bytes 3145728 | tf_op jit(solution)/shard_map/cross_kernel/pallas_call | solution.py:388
  52.0 18.3 %collective-permute-start.14 = (bf16[3,512,128]{2,1,0:T(8,128)(2,1)S(1)}, bf16[3,512,128]{2,1,0:T(8,128)(2,1)}, u32[]{:S(2)}, u32[]{:S(2)}) collective-permute-start(bf16[3,512,128]{2,1,0:T(8,128)(2,1)S(1)} %copy-done.25), channel_id=1, source_target_pairs={{0,4},{4,8},{8,12},{12,0},{1,5},{5,9},{9,13},{13,1},{2,6},{6,10},{... | collective-permute-start | bytes 1179656 | tf_op jit(solution)/shard_map/ppermute | solution.py:23
  70.3 4.8 %collective-permute-start.15 = (bf16[3,512,128]{2,1,0:T(8,128)(2,1)}, bf16[3,512,128]{2,1,0:T(8,128)(2,1)}, u32[]{:S(2)}, u32[]{:S(2)}) collective-permute-start(bf16[3,512,128]{2,1,0:T(8,128)(2,1)} %get-tuple-element.50), channel_id=1, source_target_pairs={{0,8},{4,12},{8,0},{12,4},{1,9},{5,13},{9,1},{13,5},{2,10},{6,14},... | collective-permute-start | bytes 1179656 | tf_op jit(solution)/shard_map/ppermute | solution.py:23
  75.1 3.7 %collective-permute-start.16 = (bf16[3,512,128]{2,1,0:T(8,128)(2,1)}, bf16[3,512,128]{2,1,0:T(8,128)(2,1)}, u32[]{:S(2)}, u32[]{:S(2)}) collective-permute-start(bf16[3,512,128]{2,1,0:T(8,128)(2,1)} %get-tuple-element.51), channel_id=1, source_target_pairs={{0,12},{4,0},{8,4},{12,8},{1,13},{5,1},{9,5},{13,9},{2,14},{6,2},{... | collective-permute-start | bytes 1179656 | tf_op jit(solution)/shard_map/ppermute | solution.py:23
  78.8 10.2 %attend.4 = (bf16[4,256,128]{2,1,0:T(8,128)(2,1)}, bf16[4,256,128]{2,1,0:T(8,128)(2,1)}) custom-call(s32[2]{0:T(128)} %pad_add_fusion.where_ref, bf16[1,512,1536]{2,1,0:T(8,128)(2,1)} %q_ref.6, bf16[1,512,1536]{2,1,0:T(8,128)(2,1)} %k_ref.5, bf16[1,512,1536]{2,1,0:T(8,128)(2,1)} %v_ref.5, bf16[3,512,128]{2,1,0:T(8,128)(2,1)} %copy-done.20, ...), custom_call_target="tpu_custom_call" | custom-call | flops 2147483648 | bytes 2097152 | tf_op jit(solution)/shard_map/attend/pallas_call | solution.py:119
  89.0 10.3 %collective-permute-done.1.refs_1_ = bf16[3,512,128]{2,1,0:T(8,128)(2,1)} collective-permute-done((bf16[3,512,128]{2,1,0:T(8,128)(2,1)}, bf16[3,512,128]{2,1,0:T(8,128)(2,1)}, u32[]{:S(2)}, u32[]{:S(2)}) %collective-permute-start.1) | collective-permute-done | bytes 393248 | tf_op jit(solution)/shard_map/ppermute | solution.py:23
  99.8 10.2 %attend.3 = (bf16[4,256,128]{2,1,0:T(8,128)(2,1)}, bf16[4,256,128]{2,1,0:T(8,128)(2,1)}) custom-call(s32[2]{0:T(128)} %pad_add_fusion.where_ref, bf16[1,512,1536]{2,1,0:T(8,128)(2,1)} %q_ref.6, bf16[1,512,1536]{2,1,0:T(8,128)(2,1)} %k_ref.5, bf16[1,512,1536]{2,1,0:T(8,128)(2,1)} %v_ref.5, bf16[3,512,128]{2,1,0:T(8,128)(2,1)} %copy-done.21, ...), custom_call_target="tpu_custom_call" | custom-call | flops 2147483648 | bytes 2097152 | tf_op jit(solution)/shard_map/attend/pallas_call | solution.py:119
  110.1 6.0 %collective-permute-done.15.refs_1_ = bf16[3,512,128]{2,1,0:T(8,128)(2,1)} collective-permute-done((bf16[3,512,128]{2,1,0:T(8,128)(2,1)}, bf16[3,512,128]{2,1,0:T(8,128)(2,1)}, u32[]{:S(2)}, u32[]{:S(2)}) %collective-permute-start.15) | collective-permute-done | bytes 393248 | tf_op jit(solution)/shard_map/ppermute | solution.py:23
  116.1 10.2 %attend.5 = (bf16[4,256,128]{2,1,0:T(8,128)(2,1)}, bf16[4,256,128]{2,1,0:T(8,128)(2,1)}) custom-call(s32[2]{0:T(128)} %pad_add_fusion.where_ref, bf16[1,512,1536]{2,1,0:T(8,128)(2,1)} %q_ref.6, bf16[1,512,1536]{2,1,0:T(8,128)(2,1)} %k_ref.5, bf16[1,512,1536]{2,1,0:T(8,128)(2,1)} %v_ref.5, bf16[3,512,128]{2,1,0:T(8,128)(2,1)} %collective-permute-done.14.refs_0_, ...), custom_call_target="tpu_custom_call" | custom-call | flops 2147483648 | bytes 2097152 | tf_op jit(solution)/shard_map/attend/pallas_call | solution.py:119
  127.1 2.4 %combine.4 = (bf16[256,128]{1,0:T(8,128)(2,1)}, bf16[256,128]{1,0:T(8,128)(2,1)}, bf16[256,128]{1,0:T(8,128)(2,1)}, bf16[256,128]{1,0:T(8,128)(2,1)}) custom-call(s32[2]{0:T(128)} %pad_add_fusion.where_ref, bf16[4,256,128]{2,1,0:T(8,128)(2,1)} %get-tuple-element.43.keep_ref, bf16[4,256,128]{2,1,0:T(8,128)(2,1)} %copy-done.3), custom_call_target="tpu_custom_call" | custom-call | bytes 786432 | tf_op jit(solution)/shard_map/combine/pallas_call | solution.py:152
  129.5 7.9 %collective-permute-start.11 = (bf16[256,128]{1,0:T(8,128)(2,1)}, bf16[256,128]{1,0:T(8,128)(2,1)S(1)}, u32[]{:S(2)}, u32[]{:S(2)}) collective-permute-start(bf16[256,128]{1,0:T(8,128)(2,1)} %get-tuple-element.46), channel_id=1, source_target_pairs={{0,8},{4,12},{8,0},{12,4},{1,9},{5,13},{9,1},{13,5},{2,10},{6,14},... | collective-permute-start | bytes 196616 | tf_op jit(solution)/shard_map/ppermute | solution.py:23
  137.4 3.4 %collective-permute-start.12 = (bf16[256,128]{1,0:T(8,128)(2,1)}, bf16[256,128]{1,0:T(8,128)(2,1)S(1)}, u32[]{:S(2)}, u32[]{:S(2)}) collective-permute-start(bf16[256,128]{1,0:T(8,128)(2,1)} %get-tuple-element.47), channel_id=1, source_target_pairs={{0,12},{4,0},{8,4},{12,8},{1,13},{5,1},{9,5},{13,9},{2,14},{6,2},{... | collective-permute-start | bytes 196616 | tf_op jit(solution)/shard_map/ppermute | solution.py:23
  141.5 2.5 %combine.3 = (bf16[256,128]{1,0:T(8,128)(2,1)}, bf16[256,128]{1,0:T(8,128)(2,1)}, bf16[256,128]{1,0:T(8,128)(2,1)}, bf16[256,128]{1,0:T(8,128)(2,1)}) custom-call(s32[2]{0:T(128)} %pad_add_fusion.where_ref, bf16[4,256,128]{2,1,0:T(8,128)(2,1)} %get-tuple-element.34.keep_ref, bf16[4,256,128]{2,1,0:T(8,128)(2,1)} %copy-done.2), custom_call_target="tpu_custom_call" | custom-call | bytes 786432 | tf_op jit(solution)/shard_map/combine/pallas_call | solution.py:152
  144.1 3.2 %collective-permute-start.5 = (bf16[256,128]{1,0:T(8,128)(2,1)}, bf16[256,128]{1,0:T(8,128)(2,1)S(1)}, u32[]{:S(2)}, u32[]{:S(2)}) collective-permute-start(bf16[256,128]{1,0:T(8,128)(2,1)} %get-tuple-element.38), channel_id=1, source_target_pairs={{0,12},{4,0},{8,4},{12,8},{1,13},{5,1},{9,5},{13,9},{2,14},{6,2},{... | collective-permute-start | bytes 196616 | tf_op jit(solution)/shard_map/ppermute | solution.py:23
  147.2 2.4 %combine.5 = (bf16[256,128]{1,0:T(8,128)(2,1)}, bf16[256,128]{1,0:T(8,128)(2,1)}, bf16[256,128]{1,0:T(8,128)(2,1)}, bf16[256,128]{1,0:T(8,128)(2,1)}) custom-call(s32[2]{0:T(128)} %pad_add_fusion.where_ref, bf16[4,256,128]{2,1,0:T(8,128)(2,1)} %get-tuple-element.52.keep_ref, bf16[4,256,128]{2,1,0:T(8,128)(2,1)} %copy-done.1), custom_call_target="tpu_custom_call" | custom-call | bytes 786432 | tf_op jit(solution)/shard_map/combine/pallas_call | solution.py:152
  150.2 1.5 collective-permute-start.18
  151.8 2.8 %collective-permute-start.19 = (bf16[256,128]{1,0:T(8,128)(2,1)}, bf16[256,128]{1,0:T(8,128)(2,1)S(1)}, u32[]{:S(2)}, u32[]{:S(2)}) collective-permute-start(bf16[256,128]{1,0:T(8,128)(2,1)} %get-tuple-element.56), channel_id=1, source_target_pairs={{0,12},{4,0},{8,4},{12,8},{1,13},{5,1},{9,5},{13,9},{2,14},{6,2},{... | collective-permute-start | bytes 196616 | tf_op jit(solution)/shard_map/ppermute | solution.py:23
  154.6 1.9 %collective-permute-done.6.refs_3_ = bf16[256,128]{1,0:T(8,128)(2,1)S(1)} collective-permute-done((bf16[256,128]{1,0:T(8,128)(2,1)}, bf16[256,128]{1,0:T(8,128)(2,1)S(1)}, u32[]{:S(2)}, u32[]{:S(2)}) %collective-permute-start.6) | collective-permute-done | bytes 65568 | tf_op jit(solution)/shard_map/ppermute | solution.py:23
  157.1 2.9 %assemble.1.partial_ref = bf16[256,1536]{1,0:T(8,128)(2,1)} custom-call(s32[2]{0:T(128)} %pad_add_fusion.where_ref, bf16[256,128]{1,0:T(8,128)(2,1)} %get-tuple-element.36.refs_0_, bf16[256,128]{1,0:T(8,128)(2,1)} %copy-done.12, bf16[256,128]{1,0:T(8,128)(2,1)} %copy-done.13, bf16[256,128]{1,0:T(8,128)(2,1)} %copy-done.14, ...), custom_call_target="tpu_custom_call" | custom-call | bytes 1572864 | tf_op jit(solution)/shard_map/assemble/pallas_call | solution.py:184
  161.5 2.3 %complete.1 = bf16[256,1536]{1,0:T(8,128)(2,1)} custom-call(s32[2]{0:T(128)} %pad_add_fusion.where_ref, bf16[256,1536]{1,0:T(8,128)(2,1)} %assemble.1.partial_ref, bf16[256,128]{1,0:T(8,128)(2,1)} %copy-done.15, bf16[256,128]{1,0:T(8,128)(2,1)} %copy-done.16, bf16[256,128]{1,0:T(8,128)(2,1)} %copy-done.17), custom_call_target="tpu_custom_call", output_to_operand_aliasing={{}: (1, {})} | custom-call | bytes 393216 | tf_op jit(solution)/shard_map/complete/pallas_call | solution.py:217
  (93 shorter events, 9.5 us)
Async XLA Ops:
  0.6 20.6 %collective-permute-start.21 = (bf16[1,64,1536]{2,1,0:T(8,128)(2,1)}, bf16[1,64,1536]{2,1,0:T(8,128)(2,1)S(1)}, u32[]{:S(2)}, u32[]{:S(2)}) collective-permute-start(bf16[1,64,1536]{2,1,0:T(8,128)(2,1)} %refs_1_.7), channel_id=1, source_target_pairs={{0,4},{4,8},{8,12},{1,5},{5,9},{9,13},{2,6},{6,10},{10,14},{3,7},{... | collective-permute-start | bytes 589832 | tf_op jit(solution)/shard_map/ppermute | solution.py:29
  5.6 19.4 %collective-permute-start.22 = (bf16[1,64,1536]{2,1,0:T(8,128)(2,1)}, bf16[1,64,1536]{2,1,0:T(8,128)(2,1)S(1)}, u32[]{:S(2)}, u32[]{:S(2)}) collective-permute-start(bf16[1,64,1536]{2,1,0:T(8,128)(2,1)} %refs_1_.7), channel_id=1, source_target_pairs={{4,0},{8,4},{12,8},{5,1},{9,5},{13,9},{6,2},{10,6},{14,10},{7,3},{... | collective-permute-start | bytes 589832 | tf_op jit(solution)/shard_map/ppermute | solution.py:29
  6.9 19.5 %collective-permute-start.23 = (bf16[1,64,1536]{2,1,0:T(8,128)(2,1)}, bf16[1,64,1536]{2,1,0:T(8,128)(2,1)S(1)}, u32[]{:S(2)}, u32[]{:S(2)}) collective-permute-start(bf16[1,64,1536]{2,1,0:T(8,128)(2,1)} %refs_4_.7), channel_id=1, source_target_pairs={{0,4},{4,8},{8,12},{1,5},{5,9},{9,13},{2,6},{6,10},{10,14},{3,7},{... | collective-permute-start | bytes 589832 | tf_op jit(solution)/shard_map/ppermute | solution.py:29
  15.3 18.8 %collective-permute-start.7 = (bf16[3,512,128]{2,1,0:T(8,128)(2,1)}, bf16[3,512,128]{2,1,0:T(8,128)(2,1)S(1)}, u32[]{:S(2)}, u32[]{:S(2)}) collective-permute-start(bf16[3,512,128]{2,1,0:T(8,128)(2,1)} %get-tuple-element.40), channel_id=1, source_target_pairs={{0,4},{4,8},{8,12},{12,0},{1,5},{5,9},{9,13},{13,1},{2,6},{6,10},{... | collective-permute-start | bytes 1179656 | tf_op jit(solution)/shard_map/ppermute | solution.py:23
  16.9 14.8 %collective-permute-start.24 = (bf16[1,64,1536]{2,1,0:T(8,128)(2,1)S(1)}, bf16[1,64,1536]{2,1,0:T(8,128)(2,1)S(1)}, u32[]{:S(2)}, u32[]{:S(2)}) collective-permute-start(bf16[1,64,1536]{2,1,0:T(8,128)(2,1)S(1)} %copy-done.4), channel_id=1, source_target_pairs={{4,0},{8,4},{12,8},{5,1},{9,5},{13,9},{6,2},{10,6},{14,10},{7,3},{... | collective-permute-start | bytes 589832 | tf_op jit(solution)/shard_map/ppermute | solution.py:29
  21.3 23.0 %copy-start.5 = (bf16[1,64,1536]{2,1,0:T(8,128)(2,1)}, bf16[1,64,1536]{2,1,0:T(8,128)(2,1)S(1)}, u32[]{:S(2)}) copy-start(bf16[1,64,1536]{2,1,0:T(8,128)(2,1)S(1)} %collective-permute-done.21.refs_0_) | copy-start | bytes 589828
  21.3 30.7 %collective-permute-start.8 = (bf16[3,512,128]{2,1,0:T(8,128)(2,1)}, bf16[3,512,128]{2,1,0:T(8,128)(2,1)S(1)}, u32[]{:S(2)}, u32[]{:S(2)}) collective-permute-start(bf16[3,512,128]{2,1,0:T(8,128)(2,1)} %get-tuple-element.41), channel_id=1, source_target_pairs={{0,8},{4,12},{8,0},{12,4},{1,9},{5,13},{9,1},{13,5},{2,10},{6,14},... | collective-permute-start | bytes 1179656 | tf_op jit(solution)/shard_map/ppermute | solution.py:23
  25.0 19.3 %copy-start.6 = (bf16[1,64,1536]{2,1,0:T(8,128)(2,1)}, bf16[1,64,1536]{2,1,0:T(8,128)(2,1)S(1)}, u32[]{:S(2)}) copy-start(bf16[1,64,1536]{2,1,0:T(8,128)(2,1)S(1)} %collective-permute-done.22.refs_2_) | copy-start | bytes 589828
  25.0 45.3 %collective-permute-start.9 = (bf16[3,512,128]{2,1,0:T(8,128)(2,1)S(1)}, bf16[3,512,128]{2,1,0:T(8,128)(2,1)S(1)}, u32[]{:S(2)}, u32[]{:S(2)}) collective-permute-start(bf16[3,512,128]{2,1,0:T(8,128)(2,1)S(1)} %copy-done.23), channel_id=1, source_target_pairs={{0,12},{4,0},{8,4},{12,8},{1,13},{5,1},{9,5},{13,9},{2,14},{6,2},{... | collective-permute-start | bytes 1179656 | tf_op jit(solution)/shard_map/ppermute | solution.py:23
  26.4 17.9 %copy-start.7 = (bf16[1,64,1536]{2,1,0:T(8,128)(2,1)}, bf16[1,64,1536]{2,1,0:T(8,128)(2,1)S(1)}, u32[]{:S(2)}) copy-start(bf16[1,64,1536]{2,1,0:T(8,128)(2,1)S(1)} %collective-permute-done.23.refs_3_) | copy-start | bytes 589828
  26.4 48.7 %collective-permute-start = (bf16[3,512,128]{2,1,0:T(8,128)(2,1)}, bf16[3,512,128]{2,1,0:T(8,128)(2,1)S(1)}, u32[]{:S(2)}, u32[]{:S(2)}) collective-permute-start(bf16[3,512,128]{2,1,0:T(8,128)(2,1)} %get-tuple-element.31), channel_id=1, source_target_pairs={{0,4},{4,8},{8,12},{12,0},{1,5},{5,9},{9,13},{13,1},{2,6},{6,10},{... | collective-permute-start | bytes 1179656 | tf_op jit(solution)/shard_map/ppermute | solution.py:23
  31.6 67.6 %collective-permute-start.1 = (bf16[3,512,128]{2,1,0:T(8,128)(2,1)}, bf16[3,512,128]{2,1,0:T(8,128)(2,1)}, u32[]{:S(2)}, u32[]{:S(2)}) collective-permute-start(bf16[3,512,128]{2,1,0:T(8,128)(2,1)} %get-tuple-element.32), channel_id=1, source_target_pairs={{0,8},{4,12},{8,0},{12,4},{1,9},{5,13},{9,1},{13,5},{2,10},{6,14},... | collective-permute-start | bytes 1179656 | tf_op jit(solution)/shard_map/ppermute | solution.py:23
  34.1 65.1 %collective-permute-start.2 = (bf16[3,512,128]{2,1,0:T(8,128)(2,1)}, bf16[3,512,128]{2,1,0:T(8,128)(2,1)}, u32[]{:S(2)}, u32[]{:S(2)}) collective-permute-start(bf16[3,512,128]{2,1,0:T(8,128)(2,1)} %get-tuple-element.33), channel_id=1, source_target_pairs={{0,12},{4,0},{8,4},{12,8},{1,13},{5,1},{9,5},{13,9},{2,14},{6,2},{... | collective-permute-start | bytes 1179656 | tf_op jit(solution)/shard_map/ppermute | solution.py:23
  52.0 26.8 %copy-start.22 = (bf16[3,512,128]{2,1,0:T(8,128)(2,1)}, bf16[3,512,128]{2,1,0:T(8,128)(2,1)S(1)}, u32[]{:S(2)}) copy-start(bf16[3,512,128]{2,1,0:T(8,128)(2,1)S(1)} %collective-permute-done.8.refs_1_) | copy-start | bytes 1179652
  52.0 58.0 %collective-permute-start.14 = (bf16[3,512,128]{2,1,0:T(8,128)(2,1)S(1)}, bf16[3,512,128]{2,1,0:T(8,128)(2,1)}, u32[]{:S(2)}, u32[]{:S(2)}) collective-permute-start(bf16[3,512,128]{2,1,0:T(8,128)(2,1)S(1)} %copy-done.25), channel_id=1, source_target_pairs={{0,4},{4,8},{8,12},{12,0},{1,5},{5,9},{9,13},{13,1},{2,6},{6,10},{... | collective-permute-start | bytes 1179656 | tf_op jit(solution)/shard_map/ppermute | solution.py:23
  70.3 45.8 %collective-permute-start.15 = (bf16[3,512,128]{2,1,0:T(8,128)(2,1)}, bf16[3,512,128]{2,1,0:T(8,128)(2,1)}, u32[]{:S(2)}, u32[]{:S(2)}) collective-permute-start(bf16[3,512,128]{2,1,0:T(8,128)(2,1)} %get-tuple-element.50), channel_id=1, source_target_pairs={{0,8},{4,12},{8,0},{12,4},{1,9},{5,13},{9,1},{13,5},{2,10},{6,14},... | collective-permute-start | bytes 1179656 | tf_op jit(solution)/shard_map/ppermute | solution.py:23
  75.1 13.9 %copy-start.21 = (bf16[3,512,128]{2,1,0:T(8,128)(2,1)}, bf16[3,512,128]{2,1,0:T(8,128)(2,1)S(1)}, u32[]{:S(2)}) copy-start(bf16[3,512,128]{2,1,0:T(8,128)(2,1)S(1)} %collective-permute-done.refs_0_) | copy-start | bytes 1179652
  75.1 24.2 %copy-start.19 = (bf16[256,1536]{1,0:T(8,128)(2,1)S(1)}, bf16[256,1536]{1,0:T(8,128)(2,1)}, u32[]{:S(2)}) copy-start(bf16[256,1536]{1,0:T(8,128)(2,1)} %get-tuple-element.58) | copy-start | bytes 2359300
  75.1 41.0 %collective-permute-start.16 = (bf16[3,512,128]{2,1,0:T(8,128)(2,1)}, bf16[3,512,128]{2,1,0:T(8,128)(2,1)}, u32[]{:S(2)}, u32[]{:S(2)}) collective-permute-start(bf16[3,512,128]{2,1,0:T(8,128)(2,1)} %get-tuple-element.51), channel_id=1, source_target_pairs={{0,12},{4,0},{8,4},{12,8},{1,13},{5,1},{9,5},{13,9},{2,14},{6,2},{... | collective-permute-start | bytes 1179656 | tf_op jit(solution)/shard_map/ppermute | solution.py:23
  99.3 64.5 %collective-permute-start.25 = (bf16[256,1536]{1,0:T(8,128)(2,1)S(1)}, bf16[256,1536]{1,0:T(8,128)(2,1)S(1)}, u32[]{:S(2)}, u32[]{:S(2)}) collective-permute-start(bf16[256,1536]{1,0:T(8,128)(2,1)S(1)} %copy-done.19), channel_id=1, source_target_pairs={{0,1},{1,0},{2,3},{3,2},{4,5},{5,4},{6,7},{7,6},{8,9},{9,8},{10,11... | collective-permute-start | bytes 2359304 | tf_op jit(solution)/shard_map/ppermute | solution.py:23
  99.3 27.1 %collective-permute-start.10 = (bf16[4,256,128]{2,1,0:T(8,128)(2,1)}, bf16[4,256,128]{2,1,0:T(8,128)(2,1)S(1)}, u32[]{:S(2)}, u32[]{:S(2)}) collective-permute-start(bf16[4,256,128]{2,1,0:T(8,128)(2,1)} %get-tuple-element.44), channel_id=1, source_target_pairs={{0,1},{1,0},{2,3},{3,2},{4,5},{5,4},{6,7},{7,6},{8,9},{9,8},{10,11... | collective-permute-start | bytes 786440 | tf_op jit(solution)/shard_map/ppermute | solution.py:23
  110.0 30.8 %collective-permute-start.3 = (bf16[4,256,128]{2,1,0:T(8,128)(2,1)}, bf16[4,256,128]{2,1,0:T(8,128)(2,1)S(1)}, u32[]{:S(2)}, u32[]{:S(2)}) collective-permute-start(bf16[4,256,128]{2,1,0:T(8,128)(2,1)} %get-tuple-element.35), channel_id=1, source_target_pairs={{0,1},{1,0},{2,3},{3,2},{4,5},{5,4},{6,7},{7,6},{8,9},{9,8},{10,11... | collective-permute-start | bytes 786440 | tf_op jit(solution)/shard_map/ppermute | solution.py:23
  126.3 17.7 %collective-permute-start.17 = (bf16[4,256,128]{2,1,0:T(8,128)(2,1)}, bf16[4,256,128]{2,1,0:T(8,128)(2,1)S(1)}, u32[]{:S(2)}, u32[]{:S(2)}) collective-permute-start(bf16[4,256,128]{2,1,0:T(8,128)(2,1)} %get-tuple-element.53), channel_id=1, source_target_pairs={{0,1},{1,0},{2,3},{3,2},{4,5},{5,4},{6,7},{7,6},{8,9},{9,8},{10,11... | collective-permute-start | bytes 786440 | tf_op jit(solution)/shard_map/ppermute | solution.py:23
  129.5 14.5 %collective-permute-start.11 = (bf16[256,128]{1,0:T(8,128)(2,1)}, bf16[256,128]{1,0:T(8,128)(2,1)S(1)}, u32[]{:S(2)}, u32[]{:S(2)}) collective-permute-start(bf16[256,128]{1,0:T(8,128)(2,1)} %get-tuple-element.46), channel_id=1, source_target_pairs={{0,8},{4,12},{8,0},{12,4},{1,9},{5,13},{9,1},{13,5},{2,10},{6,14},... | collective-permute-start | bytes 196616 | tf_op jit(solution)/shard_map/ppermute | solution.py:23
  137.4 12.3 %collective-permute-start.12 = (bf16[256,128]{1,0:T(8,128)(2,1)}, bf16[256,128]{1,0:T(8,128)(2,1)S(1)}, u32[]{:S(2)}, u32[]{:S(2)}) collective-permute-start(bf16[256,128]{1,0:T(8,128)(2,1)} %get-tuple-element.47), channel_id=1, source_target_pairs={{0,12},{4,0},{8,4},{12,8},{1,13},{5,1},{9,5},{13,9},{2,14},{6,2},{... | collective-permute-start | bytes 196616 | tf_op jit(solution)/shard_map/ppermute | solution.py:23
  140.8 9.4 %collective-permute-start.13 = (bf16[256,128]{1,0:T(8,128)(2,1)}, bf16[256,128]{1,0:T(8,128)(2,1)S(1)}, u32[]{:S(2)}, u32[]{:S(2)}) collective-permute-start(bf16[256,128]{1,0:T(8,128)(2,1)} %get-tuple-element.48), channel_id=1, source_target_pairs={{0,4},{4,8},{8,12},{12,0},{1,5},{5,9},{9,13},{13,1},{2,6},{6,10},{... | collective-permute-start | bytes 196616 | tf_op jit(solution)/shard_map/ppermute | solution.py:23
  144.0 7.8 %collective-permute-start.4 = (bf16[256,128]{1,0:T(8,128)(2,1)}, bf16[256,128]{1,0:T(8,128)(2,1)S(1)}, u32[]{:S(2)}, u32[]{:S(2)}) collective-permute-start(bf16[256,128]{1,0:T(8,128)(2,1)} %get-tuple-element.37), channel_id=1, source_target_pairs={{0,8},{4,12},{8,0},{12,4},{1,9},{5,13},{9,1},{13,5},{2,10},{6,14},... | collective-permute-start | bytes 196616 | tf_op jit(solution)/shard_map/ppermute | solution.py:23
  144.1 10.6 %collective-permute-start.5 = (bf16[256,128]{1,0:T(8,128)(2,1)}, bf16[256,128]{1,0:T(8,128)(2,1)S(1)}, u32[]{:S(2)}, u32[]{:S(2)}) collective-permute-start(bf16[256,128]{1,0:T(8,128)(2,1)} %get-tuple-element.38), channel_id=1, source_target_pairs={{0,12},{4,0},{8,4},{12,8},{1,13},{5,1},{9,5},{13,9},{2,14},{6,2},{... | collective-permute-start | bytes 196616 | tf_op jit(solution)/shard_map/ppermute | solution.py:23
  149.7 6.8 %collective-permute-start.6 = (bf16[256,128]{1,0:T(8,128)(2,1)}, bf16[256,128]{1,0:T(8,128)(2,1)S(1)}, u32[]{:S(2)}, u32[]{:S(2)}) collective-permute-start(bf16[256,128]{1,0:T(8,128)(2,1)} %get-tuple-element.39), channel_id=1, source_target_pairs={{0,4},{4,8},{8,12},{12,0},{1,5},{5,9},{9,13},{13,1},{2,6},{6,10},{... | collective-permute-start | bytes 196616 | tf_op jit(solution)/shard_map/ppermute | solution.py:23
  150.2 9.8 %collective-permute-start.18 = (bf16[256,128]{1,0:T(8,128)(2,1)}, bf16[256,128]{1,0:T(8,128)(2,1)S(1)}, u32[]{:S(2)}, u32[]{:S(2)}) collective-permute-start(bf16[256,128]{1,0:T(8,128)(2,1)} %get-tuple-element.55), channel_id=1, source_target_pairs={{0,8},{4,12},{8,0},{12,4},{1,9},{5,13},{9,1},{13,5},{2,10},{6,14},... | collective-permute-start | bytes 196616 | tf_op jit(solution)/shard_map/ppermute | solution.py:23
  151.8 8.3 %collective-permute-start.19 = (bf16[256,128]{1,0:T(8,128)(2,1)}, bf16[256,128]{1,0:T(8,128)(2,1)S(1)}, u32[]{:S(2)}, u32[]{:S(2)}) collective-permute-start(bf16[256,128]{1,0:T(8,128)(2,1)} %get-tuple-element.56), channel_id=1, source_target_pairs={{0,12},{4,0},{8,4},{12,8},{1,13},{5,1},{9,5},{13,9},{2,14},{6,2},{... | collective-permute-start | bytes 196616 | tf_op jit(solution)/shard_map/ppermute | solution.py:23
  154.6 6.3 %collective-permute-start.20 = (bf16[256,128]{1,0:T(8,128)(2,1)}, bf16[256,128]{1,0:T(8,128)(2,1)S(1)}, u32[]{:S(2)}, u32[]{:S(2)}) collective-permute-start(bf16[256,128]{1,0:T(8,128)(2,1)} %get-tuple-element.57), channel_id=1, source_target_pairs={{0,4},{4,8},{8,12},{12,0},{1,5},{5,9},{9,13},{13,1},{2,6},{6,10},{... | collective-permute-start | bytes 196616 | tf_op jit(solution)/shard_map/ppermute | solution.py:23
  (21 other events, 111.2 us)
where the time goes:
time: 166 us; the launch traced here: 165 us
  starting transfers between devices  75.8 us (46%)
  Pallas kernels  59.4 us (36%)
  waiting for transfers between devices  23.5 us (14%)
  local copies, waits for them, and re-layouts  2.78 us (2%)
  other arithmetic  2.57 us (2%)
    ppermute x22, starting transfers between devices, shifted(): lax.ppermute(block, axis, [(i, (i + distance) % count) for i in range(cou...  63.7 us
    pallas_call x3, Pallas kernels, attend(): pl.pallas_call(kernel, grid_spec=pltpu.PrefetchScalarGridSpec(num_scalar_...  30.5 us
    ppermute x22, waiting for transfers between devices, shifted(): lax.ppermute(block, axis, [(i, (i + distance) % count) for i in range(cou...  19 us
    ppermute x4, starting transfers between devices, neighbour(): return lax.ppermute(block, axis, route)  12.1 us
    pallas_call x3, Pallas kernels, pack(): pl.pallas_call(kernel, grid_spec=pltpu.PrefetchScalarGridSpec(num_scalar_...  9.5 us
    pallas_call x3, Pallas kernels, combine(): pl.pallas_call(kernel, grid_spec=pltpu.PrefetchScalarGridSpec(num_scalar_...  7.35 us
    pallas_call x1, Pallas kernels, cross(): call(where, allowed.astype(jnp.int32), cross_query, *sides[0], *sides[1])  6.87 us
    ppermute x4, waiting for transfers between devices, neighbour(): return lax.ppermute(block, axis, route)  4.55 us
  transfers between devices with their start and end apart: 26, of which 5 were waited for; matrix products, arithmetic and copies ran while one was open for 1% of the time, Pallas kernels for 36%

commit v1 on v0

--- a/solution.py
+++ b/solution.py
@@ -33,39 +33,6 @@
     return lax.dot_general(left, right, (((1,), (1,)), ((), ())), preferred_element_type=jnp.float32)
 
 
-def pack(where, tensors, head, heads_dest, count):
-    rows = tensors[0].shape[1]
-    kinds = len(tensors)
-
-    def kernel(where_ref, *refs):
-        ins, outs = refs[: kinds * (count - 1)], refs[kinds * (count - 1) :]
-        for k in range(count - 1):
-            for t in range(kinds):
-                outs[k][t] = ins[kinds * k + t][0]
-
-    def column(k):
-        return lambda i, w: (0, 0, ((w[0] + k) % count) * heads_dest + head)
-
-    return pl.pallas_call(
-        kernel,
-        grid_spec=pltpu.PrefetchScalarGridSpec(
-            num_scalar_prefetch=1,
-            grid=(1,),
-            in_specs=[
-                pl.BlockSpec((1, rows, DH), column(k))
-                for k in range(1, count)
-                for _ in range(kinds)
-            ],
-            out_specs=[pl.BlockSpec((kinds, rows, DH), lambda i, w: (0, 0, 0))] * (count - 1),
-        ),
-        out_shape=[jax.ShapeDtypeStruct((kinds, rows, DH), jnp.bfloat16)] * (count - 1),
-        cost_estimate=pl.CostEstimate(
-            flops=0, bytes_accessed=2 * kinds * (count - 1) * rows * DH * 2, transcendentals=0
-        ),
-        name="pack",
-    )(where, *(tuple(tensors) * (count - 1)))
-
-
 def attend(where, tensors, queries, pairs, head, heads_dest):
     rows = tensors[0].shape[1]
     count = len(pairs) + 1
@@ -76,12 +43,13 @@
     def kernel(where_ref, q_ref, k_ref, v_ref, *refs):
         pair_refs, refs = refs[: count - 1], refs[count - 1 :]
         query_refs = pair_refs if shared else refs[: count - 1]
-        keep_ref, send_ref, qs, ks, vs, sems = refs[-6:]
+        keep_ref, send_ref, qs, ks, vs, scores, sems = refs[-7:]
         column = pl.ds(pl.multiple_of((where_ref[0] * heads_dest + head) * DH, DH), DH)
 
         def fetch(r, own, other, at, scratch, sem):
             source = other[r - 1].at[at] if r else own.at[0, :, column]
-            return pltpu.make_async_copy(source, scratch.at[r * rows : (r + 1) * rows], sem)
+            target = scratch.at[r * rows : (r + 1) * rows, 0:DH]
+            return pltpu.make_async_copy(source, target, sem)
 
         key_copies = [
             fetch(r, k_ref, pair_refs, pairs[0].shape[0] - 2, ks, sems.at[0, r])
@@ -96,23 +64,32 @@
         ]
         for copy in key_copies + query_copies + value_copies:
             copy.start()
-        for copy in key_copies + query_copies + value_copies:
+        vs[:, DH:] = jnp.ones((count * rows, DH), jnp.bfloat16)
+        copy_index = where_ref[1]
+
+        def score(i, side):
+            start = i * rows + lax.rem(copy_index + side, 2) * half
+            q = qs[pl.ds(pl.multiple_of(start, half), half), :]
+            scores[side] = transposed_dot(q, ks[...])
+
+        def finish(side):
+            highest = jnp.max(scores[side], axis=1, keepdims=True)
+            expo = jnp.exp2((scores[side] - highest) * exp2_scale)
+            sums = jnp.dot(expo.astype(jnp.bfloat16), vs[...], preferred_element_type=jnp.float32)
+            return (sums[:, :DH] / sums[:, DH:]).astype(jnp.bfloat16)
+
+        for copy in key_copies + query_copies:
             copy.wait()
-        copy_index = where_ref[1]
-
-        def part(start):
-            q = qs[pl.ds(pl.multiple_of(start, half), half), :]
-            scores = transposed_dot(q, ks[...])
-            highest = jnp.max(scores, axis=1, keepdims=True)
-            expo = jnp.exp2((scores - highest) * exp2_scale)
-            denom = jnp.sum(expo, axis=1, keepdims=True)
-            numer = jnp.dot(expo.astype(jnp.bfloat16), vs[...], preferred_element_type=jnp.float32)
-            return (numer / denom).astype(jnp.bfloat16)
+        score(0, 0)
+        for copy in value_copies:
+            copy.wait()
 
         @pl.loop(0, count)
         def _(i):
-            keep_ref[i] = part(i * rows + copy_index * half)
-            send_ref[i] = part(i * rows + (1 - copy_index) * half)
+            score(i, 1)
+            keep_ref[i] = finish(0)
+            score(jnp.minimum(i + 1, count - 1), 0)
+            send_ref[i] = finish(1)
 
     tokens = count * rows
     out = pl.BlockSpec((count, half, DH), lambda i, w: (0, 0, 0))
@@ -123,8 +100,12 @@
             grid=(1,),
             in_specs=[pl.BlockSpec(memory_space=pl.ANY)] * len(operands),
             out_specs=[out, out],
-            scratch_shapes=[pltpu.VMEM((tokens, DH), jnp.bfloat16)] * 3
-            + [pltpu.SemaphoreType.DMA((3, count))],
+            scratch_shapes=[pltpu.VMEM((tokens, DH), jnp.bfloat16)] * 2
+            + [
+                pltpu.VMEM((tokens, 2 * DH), jnp.bfloat16),
+                pltpu.VMEM((2, half, tokens), jnp.float32),
+                pltpu.SemaphoreType.DMA((3, count)),
+            ],
         ),
         out_shape=[jax.ShapeDtypeStruct((count, half, DH), jnp.bfloat16)] * 2,
         cost_estimate=pl.CostEstimate(
@@ -136,138 +117,48 @@
     )(where, *operands)
 
 
-def combine(where, keep, other):
-    here, half, width = keep.shape
-
-    def kernel(where_ref, keep_ref, other_ref, *outs):
-        first = where_ref[1] == 0
-        for i in range(here):
-            mine = keep_ref[i].astype(jnp.float32)
-            theirs = other_ref[i].astype(jnp.float32)
-            cond = jnp.where(first, mine, theirs)
-            uncond = jnp.where(first, theirs, mine)
-            outs[i][...] = (uncond + guidance_weight * (cond - uncond)).astype(jnp.bfloat16)
-
-    whole = pl.BlockSpec((here, half, width), lambda i, w: (0, 0, 0))
-    return pl.pallas_call(
-        kernel,
-        grid_spec=pltpu.PrefetchScalarGridSpec(
-            num_scalar_prefetch=1,
-            grid=(1,),
-            in_specs=[whole, whole],
-            out_specs=[pl.BlockSpec((half, width), lambda i, w: (0, 0))] * here,
-        ),
-        out_shape=[jax.ShapeDtypeStruct((half, width), jnp.bfloat16)] * here,
-        cost_estimate=pl.CostEstimate(
-            flops=0, bytes_accessed=3 * here * half * width * 2, transcendentals=0
-        ),
-        name="combine",
-    )(where, keep, other)
-
-
-def column_of(where_ref, head, r, heads_dest, count):
-    column = (lax.rem(where_ref[0] + r, count) * heads_dest + head) * DH
-    return pl.ds(pl.multiple_of(column, DH), DH)
-
-
-def assemble(where, pieces, heads_dest, count):
-    places = list(pieces)
-    half = pieces[places[0]].shape[0]
-
-    def kernel(where_ref, *refs):
-        ins, out = refs[:-1], refs[-1]
-        for place, ref in zip(places, ins):
-            out[:, column_of(where_ref, *place, heads_dest, count)] = ref[...]
-
-    block = pl.BlockSpec((half, DH), lambda i, w: (0, 0))
-    width = heads_dest * count * DH
-    return pl.pallas_call(
-        kernel,
-        grid_spec=pltpu.PrefetchScalarGridSpec(
-            num_scalar_prefetch=1,
-            grid=(1,),
-            in_specs=[block] * len(places),
-            out_specs=pl.BlockSpec((half, width), lambda i, w: (0, 0)),
-        ),
-        out_shape=jax.ShapeDtypeStruct((half, width), jnp.bfloat16),
-        cost_estimate=pl.CostEstimate(
-            flops=0, bytes_accessed=2 * half * width * 2, transcendentals=0
-        ),
-        name="assemble",
-    )(where, *pieces.values())
-
-
-def complete(where, partial, pieces, heads_dest, count):
-    places = list(pieces)
-    half, width = partial.shape
-
-    def kernel(where_ref, partial_ref, *refs):
-        ins, out, sems = refs[:-2], refs[-2], refs[-1]
-        copies = [
-            pltpu.make_async_copy(
-                ref, out.at[:, column_of(where_ref, *place, heads_dest, count)], sems.at[i]
-            )
-            for i, (place, ref) in enumerate(zip(places, ins))
-        ]
-        for copy in copies:
-            copy.start()
-        for copy in copies:
-            copy.wait()
-
-    return pl.pallas_call(
-        kernel,
-        grid_spec=pltpu.PrefetchScalarGridSpec(
-            num_scalar_prefetch=1,
-            grid=(1,),
-            in_specs=[pl.BlockSpec(memory_space=pl.ANY)]
-            + [pl.BlockSpec((half, DH), lambda i, w: (0, 0))] * len(places),
-            out_specs=pl.BlockSpec(memory_space=pl.ANY),
-            scratch_shapes=[pltpu.SemaphoreType.DMA((len(places),))],
-        ),
-        out_shape=jax.ShapeDtypeStruct((half, width), jnp.bfloat16),
-        input_output_aliases={1: 0},
-        cost_estimate=pl.CostEstimate(
-            flops=0, bytes_accessed=2 * half * DH * len(places) * 2, transcendentals=0
-        ),
-        name="complete",
-    )(where, partial, *pieces.values())
-
-
-def send_order(count):
-    return sorted(range(1, count), key=lambda k: -min(k, count - k))
-
-
 def self_by_heads(where, video_query, video_key, video_value):
     count = lax.axis_size("seq")
+    here = lax.axis_index("seq")
     heads_dest = video_query.shape[2] // DH // count
+    half = video_query.shape[1] // 2
     tensors = (video_query, video_key, video_value)
-    order = send_order(count)
-    last = heads_dest - 1
-
-    def inflow(kinds, head):
-        sent = pack(where, kinds, head, heads_dest, count)
-        received = [None] * (count - 1)
-        for k in order:
-            received[k - 1] = shifted(sent[k - 1], "seq", k)
-        return received
-
-    def outflow(queries, pairs, head):
-        keep, send = attend(where, tensors, queries, pairs, head, heads_dest)
-        other = shifted(send, "branch", 1)
-        guided = combine(where, keep, other)
-        done = {(head, 0): guided[0]}
-        for r in order:
-            done[head, r] = shifted(guided[r], "seq", -r)
-        return done
-
-    received = [inflow(tensors, head) for head in range(heads_dest)]
-    pieces = {}
-    for head in range(last):
-        pieces |= outflow(received[head], received[head], head)
-    final = outflow(received[last], received[last], last)
-    pieces[last, 0] = final.pop((last, 0))
-    partial = assemble(where, pieces, heads_dest, count)
-    return complete(where, partial, final, heads_dest, count)
+
+    def column(steps, head):
+        return ((here + steps) % count * heads_dest + head) * DH
+
+    received = []
+    for head in range(heads_dest):
+        slots = []
+        for k in range(1, count):
+            sent = jnp.concatenate(
+                [lax.dynamic_slice_in_dim(t, column(k, head), DH, 2) for t in tensors]
+            )
+            if head == 0 and k == 1:
+                sent, *tensors = lax.optimization_barrier((sent, *tensors))
+            slots.append(shifted(sent, "seq", k))
+        received.append(slots)
+    pieces = []
+    for heads in (range(heads_dest - 1), [heads_dest - 1]):
+        keeps, others = [], []
+        for head in heads:
+            keep, send = attend(where, tensors, received[head], received[head], head, heads_dest)
+            others.append(shifted(send, "branch", 1))
+            keeps.append(keep)
+        for k in range(count) if heads else ():
+            rows = jnp.concatenate(
+                [guide(keep[k], other[k]) for keep, other in zip(keeps, others)], axis=1
+            )
+            if k:
+                rows = shifted(rows, "seq", -k)
+            pieces.append((k > 0, column(k, heads[0]), rows))
+    out = jnp.zeros((half, video_query.shape[2]), jnp.bfloat16)
+    out, _ = lax.optimization_barrier((out, others[-1]))
+    for remote in (False, True):
+        for moved, start, rows in pieces:
+            if moved == remote:
+                out = lax.dynamic_update_slice_in_dim(out, rows, start, 1)
+    return out
 
 
 def self_by_rows(video_query, video_key, video_value):
@@ -396,7 +287,8 @@
     where = jnp.stack([lax.axis_index("seq"), lax.axis_index("branch")]).astype(jnp.int32)
     heads_dev = video_query.shape[2] // DH
     guided_cross = cross(where, cross_query, audio_key, audio_value, tile_list, tile_count)
-    if heads_dev % lax.axis_size("seq") == 0:
+    count = lax.axis_size("seq")
+    if heads_dev % count == 0:
         guided_self = self_by_heads(where, video_query, video_key, video_value)
     else:
         guided_self = self_by_rows(video_query, video_key, video_value)

time: 166 us -> 158 us (0.952)
  Pallas kernels: 59.4 us -> 33.8 us
  waiting for transfers between devices: 23.5 us -> 42.9 us
  starting transfers between devices: 75.8 us -> 68.6 us
  other arithmetic: 2.57 us -> 5.78 us
  local copies, waits for them, and re-layouts: 2.78 us -> 5.18 us
    ppermute x22 -> x19, waiting for transfers between devices: 19 us -> 42.9 us  [shifted(): lax.ppermute(block, axis, [(i, (i + distance) % count) for i in range(cou...]
    pallas_call x8 -> x0, Pallas kernels: 22 us -> none  [the longest x3 9.5 us: pack(): pl.pallas_call(kernel, grid_spec=pltpu.PrefetchScalarGridSpec(num_scalar_...]
    ppermute x22 -> x19, starting transfers between devices: 63.7 us -> 55 us  [shifted(): lax.ppermute(block, axis, [(i, (i + distance) % count) for i in range(cou...]
    ppermute x4, waiting for transfers between devices: 4.55 us -> 0.01 us  [neighbour(): return lax.ppermute(block, axis, route)]
    pallas_call x3, Pallas kernels: 30.5 us -> 26.8 us  [attend(): pl.pallas_call(kernel, grid_spec=pltpu.PrefetchScalarGridSpec(num_scalar_...]
    dynamic_slice x0 -> x5, local copies, waits for them, and re-layouts: none -> 3.14 us  [self_by_heads(): lax.dynamic_slice_in_dim(t, column(k, head), DH, 2)]
    concatenate x0 -> x12, other arithmetic: none -> 2.7 us  [the longest x9 2.65 us: self_by_heads(): jnp.concatenate([lax.dynamic_slice_in_dim(t, column(k, head), DH, 2) for...]
  transfers between devices with their start and end apart: 26 -> 23, of which waited for: 5 -> 6; matrix products, arithmetic and copies ran while one was open for 1% -> 5% of each run, Pallas kernels for 36% -> 21%
where the time goes in v1:
time: 158 us; the launch traced here: 157 us
  starting transfers between devices  68.6 us (43%)
  waiting for transfers between devices  42.9 us (27%)
  Pallas kernels  33.8 us (21%)
  other arithmetic  5.78 us (4%)
  local copies, waits for them, and re-layouts  5.18 us (3%)
    ppermute x19, starting transfers between devices, shifted(): lax.ppermute(block, axis, [(i, (i + distance) % count) for i in range(cou...  55 us
    ppermute x19, waiting for transfers between devices, shifted(): lax.ppermute(block, axis, [(i, (i + distance) % count) for i in range(cou...  42.9 us
    pallas_call x3, Pallas kernels, attend(): pl.pallas_call(kernel, grid_spec=pltpu.PrefetchScalarGridSpec(num_scalar_...  26.8 us
    ppermute x4, starting transfers between devices, neighbour(): return lax.ppermute(block, axis, route)  13.6 us
    pallas_call x1, Pallas kernels, cross(): call(where, allowed.astype(jnp.int32), cross_query, *sides[0], *sides[1])  7.06 us
  transfers between devices with their start and end apart: 23, of which 6 were waited for; matrix products, arithmetic and copies ran while one was open for 5% of the time, Pallas kernels for 21%

profile of v1, /device:TPU:0, one launch (start us, length us, event | category | flops | bytes accessed | tf_op | source)
XLA Modules:
  0.0 157.4 jit_solution(5983794547120948831)
XLA Ops:
  0.6 5.8 %collective-permute-start.18 = (bf16[1,64,1536]{2,1,0:T(8,128)(2,1)}, bf16[1,64,1536]{2,1,0:T(8,128)(2,1)}, u32[]{:S(2)}, u32[]{:S(2)}) collective-permute-start(bf16[1,64,1536]{2,1,0:T(8,128)(2,1)} %refs_1_.1), channel_id=1, source_target_pairs={{0,4},{4,8},{8,12},{1,5},{5,9},{9,13},{2,6},{6,10},{10,14},{3,7},{... | collective-permute-start | bytes 589832 | tf_op jit(solution)/shard_map/ppermute | solution.py:29
  6.4 1.3 collective-permute-start.19
  7.7 5.2 %collective-permute-start.20 = (bf16[1,64,1536]{2,1,0:T(8,128)(2,1)}, bf16[1,64,1536]{2,1,0:T(8,128)(2,1)}, u32[]{:S(2)}, u32[]{:S(2)}) collective-permute-start(bf16[1,64,1536]{2,1,0:T(8,128)(2,1)} %refs_4_.1), channel_id=1, source_target_pairs={{0,4},{4,8},{8,12},{1,5},{5,9},{9,13},{2,6},{6,10},{10,14},{3,7},{... | collective-permute-start | bytes 589832 | tf_op jit(solution)/shard_map/ppermute | solution.py:29
  12.9 1.3 collective-permute-start.21
  14.3 0.9 constant_dynamic-slice_fusion.26
  15.2 1.0 constant_dynamic-slice_fusion.24
  16.2 0.8 pad_maximum_fusion
  17.8 0.8 constant_dynamic-slice_fusion.10
  19.4 0.8 pad_maximum_fusion.4
  20.2 2.6 %collective-permute-start.5 = (bf16[3,512,128]{2,1,0:T(8,128)(2,1)}, bf16[3,512,128]{2,1,0:T(8,128)(2,1)}, u32[]{:S(2)}, u32[]{:S(2)}) collective-permute-start(bf16[3,512,128]{2,1,0:T(8,128)(2,1)} %pad_maximum_fusion.4), channel_id=1, source_target_pairs={{0,8},{4,12},{8,0},{12,4},{1,9},{5,13},{9,1},{13,5},{2,10},{6,14},... | collective-permute-start | bytes 1179656 | tf_op jit(solution)/shard_map/ppermute | solution.py:23
  23.8 2.5 %collective-permute-start.6 = (bf16[3,512,128]{2,1,0:T(8,128)(2,1)S(1)}, bf16[3,512,128]{2,1,0:T(8,128)(2,1)}, u32[]{:S(2)}, u32[]{:S(2)}) collective-permute-start(bf16[3,512,128]{2,1,0:T(8,128)(2,1)S(1)} %pad_maximum_fusion.5), channel_id=1, source_target_pairs={{0,12},{4,0},{8,4},{12,8},{1,13},{5,1},{9,5},{13,9},{2,14},{6,2},{... | collective-permute-start | bytes 1179656 | tf_op jit(solution)/shard_map/ppermute | solution.py:23
  26.6 3.6 %collective-permute-start.10 = (bf16[3,512,128]{2,1,0:T(8,128)(2,1)S(1)}, bf16[3,512,128]{2,1,0:T(8,128)(2,1)}, u32[]{:S(2)}, u32[]{:S(2)}) collective-permute-start(bf16[3,512,128]{2,1,0:T(8,128)(2,1)S(1)} %pad_maximum_fusion.8), channel_id=1, source_target_pairs={{0,12},{4,0},{8,4},{12,8},{1,13},{5,1},{9,5},{13,9},{2,14},{6,2},{... | collective-permute-start | bytes 1179656 | tf_op jit(solution)/shard_map/ppermute | solution.py:23
  30.3 13.7 %collective-permute-done.5.refs_1_ = bf16[3,512,128]{2,1,0:T(8,128)(2,1)} collective-permute-done((bf16[3,512,128]{2,1,0:T(8,128)(2,1)}, bf16[3,512,128]{2,1,0:T(8,128)(2,1)}, u32[]{:S(2)}, u32[]{:S(2)}) %collective-permute-start.5) | collective-permute-done | bytes 393248 | tf_op jit(solution)/shard_map/ppermute | solution.py:23
  44.0 6.7 %collective-permute-start.8 = (bf16[3,512,128]{2,1,0:T(8,128)(2,1)S(1)}, bf16[3,512,128]{2,1,0:T(8,128)(2,1)}, u32[]{:S(2)}, u32[]{:S(2)}) collective-permute-start(bf16[3,512,128]{2,1,0:T(8,128)(2,1)S(1)} %pad_maximum_fusion.6), channel_id=1, source_target_pairs={{0,4},{4,8},{8,12},{12,0},{1,5},{5,9},{9,13},{13,1},{2,6},{6,10},{... | collective-permute-start | bytes 1179656 | tf_op jit(solution)/shard_map/ppermute | solution.py:23
  52.0 0.8 pad_maximum_fusion.1
  52.8 7.1 %cross_kernel.1 = (bf16[256,1536]{1,0:T(8,128)(2,1)}, bf16[256,1536]{1,0:T(8,128)(2,1)}) custom-call(s32[2]{0:T(128)} %pad_add_fusion.where_ref, s32[4,192]{1,0:T(4,128)} %convert_element_type.252.allowed_ref, bf16[1,512,1536]{2,1,0:T(8,128)(2,1)} %q_ref.4, bf16[1,64,1536]{2,1,0:T(8,128)(2,1)} %collective-permute-done.18.refs_0_, ...), custom_call_target="tpu_custom_call" | custom-call | flops 603979776 | bytes 3145728 | tf_op jit(solution)/shard_map/cross_kernel/pallas_call | solution.py:279
  59.9 3.2 %collective-permute-start.2 = (bf16[3,512,128]{2,1,0:T(8,128)(2,1)S(1)}, bf16[3,512,128]{2,1,0:T(8,128)(2,1)S(1)}, u32[]{:S(2)}, u32[]{:S(2)}) collective-permute-start(bf16[3,512,128]{2,1,0:T(8,128)(2,1)S(1)} %pad_maximum_fusion.3), channel_id=1, source_target_pairs={{0,12},{4,0},{8,4},{12,8},{1,13},{5,1},{9,5},{13,9},{2,14},{6,2},{... | collective-permute-start | bytes 1179656 | tf_op jit(solution)/shard_map/ppermute | solution.py:23
  63.0 15.2 %collective-permute-start.1 = (bf16[3,512,128]{2,1,0:T(8,128)(2,1)S(1)}, bf16[3,512,128]{2,1,0:T(8,128)(2,1)}, u32[]{:S(2)}, u32[]{:S(2)}) collective-permute-start(bf16[3,512,128]{2,1,0:T(8,128)(2,1)S(1)} %pad_maximum_fusion.2), channel_id=1, source_target_pairs={{0,8},{4,12},{8,0},{12,4},{1,9},{5,13},{9,1},{13,5},{2,10},{6,14},... | collective-permute-start | bytes 1179656 | tf_op jit(solution)/shard_map/ppermute | solution.py:23
  78.3 8.4 %collective-permute-start = (bf16[3,512,128]{2,1,0:T(8,128)(2,1)S(1)}, bf16[3,512,128]{2,1,0:T(8,128)(2,1)}, u32[]{:S(2)}, u32[]{:S(2)}) collective-permute-start(bf16[3,512,128]{2,1,0:T(8,128)(2,1)S(1)} %copy-done.7), channel_id=1, source_target_pairs={{0,4},{4,8},{8,12},{12,0},{1,5},{5,9},{9,13},{13,1},{2,6},{6,10},{... | collective-permute-start | bytes 1179656 | tf_op jit(solution)/shard_map/ppermute | solution.py:23
  86.7 8.9 %attend.4 = (bf16[4,256,128]{2,1,0:T(8,128)(2,1)}, bf16[4,256,128]{2,1,0:T(8,128)(2,1)}) custom-call(s32[2]{0:T(128)} %pad_add_fusion.where_ref, bf16[1,512,1536]{2,1,0:T(8,128)(2,1)} %q_ref.3, bf16[1,512,1536]{2,1,0:T(8,128)(2,1)} %k_ref.2, bf16[1,512,1536]{2,1,0:T(8,128)(2,1)} %v_ref.2, bf16[3,512,128]{2,1,0:T(8,128)(2,1)} %collective-permute-done.4.refs_0_, ...), custom_call_target="tpu_custom_call" | custom-call | flops 2147483648 | bytes 2097152 | tf_op jit(solution)/shard_map/attend/pallas_call | solution.py:96
  95.6 13.6 %collective-permute-done.9.refs_1_ = bf16[3,512,128]{2,1,0:T(8,128)(2,1)} collective-permute-done((bf16[3,512,128]{2,1,0:T(8,128)(2,1)S(1)}, bf16[3,512,128]{2,1,0:T(8,128)(2,1)}, u32[]{:S(2)}, u32[]{:S(2)}) %collective-permute-start.9) | collective-permute-done | bytes 393248 | tf_op jit(solution)/shard_map/ppermute | solution.py:23
  109.8 8.9 %attend.5 = (bf16[4,256,128]{2,1,0:T(8,128)(2,1)}, bf16[4,256,128]{2,1,0:T(8,128)(2,1)}) custom-call(s32[2]{0:T(128)} %pad_add_fusion.where_ref, bf16[1,512,1536]{2,1,0:T(8,128)(2,1)} %q_ref.3, bf16[1,512,1536]{2,1,0:T(8,128)(2,1)} %k_ref.2, bf16[1,512,1536]{2,1,0:T(8,128)(2,1)} %v_ref.2, bf16[3,512,128]{2,1,0:T(8,128)(2,1)} %collective-permute-done.8.refs_0_, ...), custom_call_target="tpu_custom_call" | custom-call | flops 2147483648 | bytes 2097152 | tf_op jit(solution)/shard_map/attend/pallas_call | solution.py:96
  118.8 5.4 %collective-permute-done.1.refs_1_ = bf16[3,512,128]{2,1,0:T(8,128)(2,1)} collective-permute-done((bf16[3,512,128]{2,1,0:T(8,128)(2,1)S(1)}, bf16[3,512,128]{2,1,0:T(8,128)(2,1)}, u32[]{:S(2)}, u32[]{:S(2)}) %collective-permute-start.1) | collective-permute-done | bytes 393248 | tf_op jit(solution)/shard_map/ppermute | solution.py:23
  124.2 8.9 %attend.3 = (bf16[4,256,128]{2,1,0:T(8,128)(2,1)}, bf16[4,256,128]{2,1,0:T(8,128)(2,1)}) custom-call(s32[2]{0:T(128)} %pad_add_fusion.where_ref, bf16[1,512,1536]{2,1,0:T(8,128)(2,1)} %q_ref.3, bf16[1,512,1536]{2,1,0:T(8,128)(2,1)} %k_ref.2, bf16[1,512,1536]{2,1,0:T(8,128)(2,1)} %v_ref.2, bf16[3,512,128]{2,1,0:T(8,128)(2,1)} %collective-permute-done.refs_0_, ...), custom_call_target="tpu_custom_call" | custom-call | flops 2147483648 | bytes 2097152 | tf_op jit(solution)/shard_map/attend/pallas_call | solution.py:96
  134.2 2.1 %collective-permute-start.13 = (bf16[256,256]{1,0:T(8,128)(2,1)S(1)}, bf16[256,256]{1,0:T(8,128)(2,1)S(1)}, u32[]{:S(2)}, u32[]{:S(2)}) collective-permute-start(bf16[256,256]{1,0:T(8,128)(2,1)S(1)} %pad_maximum_fusion.10), channel_id=1, source_target_pairs={{0,8},{4,12},{8,0},{12,4},{1,9},{5,13},{9,1},{13,5},{2,10},{6,14},... | collective-permute-start | bytes 393224 | tf_op jit(solution)/shard_map/ppermute | solution.py:23
  136.3 3.0 %collective-permute-start.12 = (bf16[256,256]{1,0:T(8,128)(2,1)S(1)}, bf16[256,256]{1,0:T(8,128)(2,1)S(1)}, u32[]{:S(2)}, u32[]{:S(2)}) collective-permute-start(bf16[256,256]{1,0:T(8,128)(2,1)S(1)} %pad_maximum_fusion.9), channel_id=1, source_target_pairs={{0,12},{4,0},{8,4},{12,8},{1,13},{5,1},{9,5},{13,9},{2,14},{6,2},{... | collective-permute-start | bytes 393224 | tf_op jit(solution)/shard_map/ppermute | solution.py:23
  139.6 5.1 %collective-permute-done.12 = bf16[256,256]{1,0:T(8,128)(2,1)S(1)} collective-permute-done((bf16[256,256]{1,0:T(8,128)(2,1)S(1)}, bf16[256,256]{1,0:T(8,128)(2,1)S(1)}, u32[]{:S(2)}, u32[]{:S(2)}) %collective-permute-start.12) | collective-permute-done | bytes 131104 | tf_op jit(solution)/shard_map/ppermute | solution.py:23
  144.7 4.7 %collective-permute-start.16 = (bf16[256,128]{1,0:T(8,128)(2,1)S(1)}, bf16[256,128]{1,0:T(8,128)(2,1)S(1)}, u32[]{:S(2)}, u32[]{:S(2)}) collective-permute-start(bf16[256,128]{1,0:T(8,128)(2,1)S(1)} %get-tuple-element.53), channel_id=1, source_target_pairs={{0,8},{4,12},{8,0},{12,4},{1,9},{5,13},{9,1},{13,5},{2,10},{6,14},... | collective-permute-start | bytes 196616 | tf_op jit(solution)/shard_map/ppermute | solution.py:23
  149.5 1.4 collective-permute-start.17
  150.9 1.1 collective-permute-done.16
  152.1 4.0 %collective-permute-done.17 = bf16[256,128]{1,0:T(8,128)(2,1)S(1)} collective-permute-done((bf16[256,128]{1,0:T(8,128)(2,1)S(1)}, bf16[256,128]{1,0:T(8,128)(2,1)S(1)}, u32[]{:S(2)}, u32[]{:S(2)}) %collective-permute-start.17) | collective-permute-done | bytes 65568 | tf_op jit(solution)/shard_map/ppermute | solution.py:23
  156.1 1.3 fusion.1
  (82 shorter events, 6.2 us)
Async XLA Ops:
  0.6 16.4 %copy-start = (bf16[1,512,1536]{2,1,0:T(8,128)(2,1)S(1)}, bf16[1,512,1536]{2,1,0:T(8,128)(2,1)}, u32[]{:S(2)}) copy-start(bf16[1,512,1536]{2,1,0:T(8,128)(2,1)} %q_ref.3) | copy-start | bytes 4718596
  0.6 23.2 %collective-permute-start.18 = (bf16[1,64,1536]{2,1,0:T(8,128)(2,1)}, bf16[1,64,1536]{2,1,0:T(8,128)(2,1)}, u32[]{:S(2)}, u32[]{:S(2)}) collective-permute-start(bf16[1,64,1536]{2,1,0:T(8,128)(2,1)} %refs_1_.1), channel_id=1, source_target_pairs={{0,4},{4,8},{8,12},{1,5},{5,9},{9,13},{2,6},{6,10},{10,14},{3,7},{... | collective-permute-start | bytes 589832 | tf_op jit(solution)/shard_map/ppermute | solution.py:29
  6.4 19.9 %collective-permute-start.19 = (bf16[1,64,1536]{2,1,0:T(8,128)(2,1)}, bf16[1,64,1536]{2,1,0:T(8,128)(2,1)}, u32[]{:S(2)}, u32[]{:S(2)}) collective-permute-start(bf16[1,64,1536]{2,1,0:T(8,128)(2,1)} %refs_1_.1), channel_id=1, source_target_pairs={{4,0},{8,4},{12,8},{5,1},{9,5},{13,9},{6,2},{10,6},{14,10},{7,3},{... | collective-permute-start | bytes 589832 | tf_op jit(solution)/shard_map/ppermute | solution.py:29
  7.7 18.9 %collective-permute-start.20 = (bf16[1,64,1536]{2,1,0:T(8,128)(2,1)}, bf16[1,64,1536]{2,1,0:T(8,128)(2,1)}, u32[]{:S(2)}, u32[]{:S(2)}) collective-permute-start(bf16[1,64,1536]{2,1,0:T(8,128)(2,1)} %refs_4_.1), channel_id=1, source_target_pairs={{0,4},{4,8},{8,12},{1,5},{5,9},{9,13},{2,6},{6,10},{10,14},{3,7},{... | collective-permute-start | bytes 589832 | tf_op jit(solution)/shard_map/ppermute | solution.py:29
  12.9 17.3 %collective-permute-start.21 = (bf16[1,64,1536]{2,1,0:T(8,128)(2,1)}, bf16[1,64,1536]{2,1,0:T(8,128)(2,1)}, u32[]{:S(2)}, u32[]{:S(2)}) collective-permute-start(bf16[1,64,1536]{2,1,0:T(8,128)(2,1)} %refs_4_.1), channel_id=1, source_target_pairs={{4,0},{8,4},{12,8},{5,1},{9,5},{13,9},{6,2},{10,6},{14,10},{7,3},{... | collective-permute-start | bytes 589832 | tf_op jit(solution)/shard_map/ppermute | solution.py:29
  19.2 3.5 %copy-start.13 = (s32[4]{0:T(128)S(1)}, s32[4]{0:T(128)}, u32[]{:S(2)}) copy-start(s32[4]{0:T(128)} %param.15) | copy-start | bytes 52
  20.2 23.8 %collective-permute-start.5 = (bf16[3,512,128]{2,1,0:T(8,128)(2,1)}, bf16[3,512,128]{2,1,0:T(8,128)(2,1)}, u32[]{:S(2)}, u32[]{:S(2)}) collective-permute-start(bf16[3,512,128]{2,1,0:T(8,128)(2,1)} %pad_maximum_fusion.4), channel_id=1, source_target_pairs={{0,8},{4,12},{8,0},{12,4},{1,9},{5,13},{9,1},{13,5},{2,10},{6,14},... | collective-permute-start | bytes 1179656 | tf_op jit(solution)/shard_map/ppermute | solution.py:23
  22.9 3.4 %copy-start.6 = (bf16[3,512,128]{2,1,0:T(8,128)(2,1)S(1)}, bf16[3,512,128]{2,1,0:T(8,128)(2,1)}, u32[]{:S(2)}) copy-start(bf16[3,512,128]{2,1,0:T(8,128)(2,1)} %pad_maximum_fusion) | copy-start | bytes 1179652
  23.8 36.0 %collective-permute-start.6 = (bf16[3,512,128]{2,1,0:T(8,128)(2,1)S(1)}, bf16[3,512,128]{2,1,0:T(8,128)(2,1)}, u32[]{:S(2)}, u32[]{:S(2)}) collective-permute-start(bf16[3,512,128]{2,1,0:T(8,128)(2,1)S(1)} %pad_maximum_fusion.5), channel_id=1, source_target_pairs={{0,12},{4,0},{8,4},{12,8},{1,13},{5,1},{9,5},{13,9},{2,14},{6,2},{... | collective-permute-start | bytes 1179656 | tf_op jit(solution)/shard_map/ppermute | solution.py:23
  26.3 36.7 %collective-permute-start.4 = (bf16[3,512,128]{2,1,0:T(8,128)(2,1)S(1)}, bf16[3,512,128]{2,1,0:T(8,128)(2,1)}, u32[]{:S(2)}, u32[]{:S(2)}) collective-permute-start(bf16[3,512,128]{2,1,0:T(8,128)(2,1)S(1)} %copy-done.6), channel_id=1, source_target_pairs={{0,4},{4,8},{8,12},{12,0},{1,5},{5,9},{9,13},{13,1},{2,6},{6,10},{... | collective-permute-start | bytes 1179656 | tf_op jit(solution)/shard_map/ppermute | solution.py:23
  26.6 51.7 %collective-permute-start.10 = (bf16[3,512,128]{2,1,0:T(8,128)(2,1)S(1)}, bf16[3,512,128]{2,1,0:T(8,128)(2,1)}, u32[]{:S(2)}, u32[]{:S(2)}) collective-permute-start(bf16[3,512,128]{2,1,0:T(8,128)(2,1)S(1)} %pad_maximum_fusion.8), channel_id=1, source_target_pairs={{0,12},{4,0},{8,4},{12,8},{1,13},{5,1},{9,5},{13,9},{2,14},{6,2},{... | collective-permute-start | bytes 1179656 | tf_op jit(solution)/shard_map/ppermute | solution.py:23
  30.3 79.0 %collective-permute-start.9 = (bf16[3,512,128]{2,1,0:T(8,128)(2,1)S(1)}, bf16[3,512,128]{2,1,0:T(8,128)(2,1)}, u32[]{:S(2)}, u32[]{:S(2)}) collective-permute-start(bf16[3,512,128]{2,1,0:T(8,128)(2,1)S(1)} %pad_maximum_fusion.7), channel_id=1, source_target_pairs={{0,8},{4,12},{8,0},{12,4},{1,9},{5,13},{9,1},{13,5},{2,10},{6,14},... | collective-permute-start | bytes 1179656 | tf_op jit(solution)/shard_map/ppermute | solution.py:23
  44.0 65.2 %collective-permute-start.8 = (bf16[3,512,128]{2,1,0:T(8,128)(2,1)S(1)}, bf16[3,512,128]{2,1,0:T(8,128)(2,1)}, u32[]{:S(2)}, u32[]{:S(2)}) collective-permute-start(bf16[3,512,128]{2,1,0:T(8,128)(2,1)S(1)} %pad_maximum_fusion.6), channel_id=1, source_target_pairs={{0,4},{4,8},{8,12},{12,0},{1,5},{5,9},{9,13},{13,1},{2,6},{6,10},{... | collective-permute-start | bytes 1179656 | tf_op jit(solution)/shard_map/ppermute | solution.py:23
  52.8 25.5 %copy-start.7 = (bf16[3,512,128]{2,1,0:T(8,128)(2,1)S(1)}, bf16[3,512,128]{2,1,0:T(8,128)(2,1)}, u32[]{:S(2)}) copy-start(bf16[3,512,128]{2,1,0:T(8,128)(2,1)} %pad_maximum_fusion.1) | copy-start | bytes 1179652
  59.9 58.8 %collective-permute-start.2 = (bf16[3,512,128]{2,1,0:T(8,128)(2,1)S(1)}, bf16[3,512,128]{2,1,0:T(8,128)(2,1)S(1)}, u32[]{:S(2)}, u32[]{:S(2)}) collective-permute-start(bf16[3,512,128]{2,1,0:T(8,128)(2,1)S(1)} %pad_maximum_fusion.3), channel_id=1, source_target_pairs={{0,12},{4,0},{8,4},{12,8},{1,13},{5,1},{9,5},{13,9},{2,14},{6,2},{... | collective-permute-start | bytes 1179656 | tf_op jit(solution)/shard_map/ppermute | solution.py:23
  63.0 61.1 %collective-permute-start.1 = (bf16[3,512,128]{2,1,0:T(8,128)(2,1)S(1)}, bf16[3,512,128]{2,1,0:T(8,128)(2,1)}, u32[]{:S(2)}, u32[]{:S(2)}) collective-permute-start(bf16[3,512,128]{2,1,0:T(8,128)(2,1)S(1)} %pad_maximum_fusion.2), channel_id=1, source_target_pairs={{0,8},{4,12},{8,0},{12,4},{1,9},{5,13},{9,1},{13,5},{2,10},{6,14},... | collective-permute-start | bytes 1179656 | tf_op jit(solution)/shard_map/ppermute | solution.py:23
  78.3 45.9 %collective-permute-start = (bf16[3,512,128]{2,1,0:T(8,128)(2,1)S(1)}, bf16[3,512,128]{2,1,0:T(8,128)(2,1)}, u32[]{:S(2)}, u32[]{:S(2)}) collective-permute-start(bf16[3,512,128]{2,1,0:T(8,128)(2,1)S(1)} %copy-done.7), channel_id=1, source_target_pairs={{0,4},{4,8},{8,12},{12,0},{1,5},{5,9},{9,13},{13,1},{2,6},{6,10},{... | collective-permute-start | bytes 1179656 | tf_op jit(solution)/shard_map/ppermute | solution.py:23
  109.2 46.9 %collective-permute-start.22 = (bf16[256,1536]{1,0:T(8,128)(2,1)}, bf16[256,1536]{1,0:T(8,128)(2,1)S(1)}, u32[]{:S(2)}, u32[]{:S(2)}) collective-permute-start(bf16[256,1536]{1,0:T(8,128)(2,1)} %get-tuple-element.26), channel_id=1, source_target_pairs={{0,1},{1,0},{2,3},{3,2},{4,5},{5,4},{6,7},{7,6},{8,9},{9,8},{10,11... | collective-permute-start | bytes 2359304 | tf_op jit(solution)/shard_map/ppermute | solution.py:23
  109.2 24.0 %collective-permute-start.7 = (bf16[4,256,128]{2,1,0:T(8,128)(2,1)}, bf16[4,256,128]{2,1,0:T(8,128)(2,1)S(1)}, u32[]{:S(2)}, u32[]{:S(2)}) collective-permute-start(bf16[4,256,128]{2,1,0:T(8,128)(2,1)} %get-tuple-element.21), channel_id=1, source_target_pairs={{0,1},{1,0},{2,3},{3,2},{4,5},{5,4},{6,7},{7,6},{8,9},{9,8},{10,11... | collective-permute-start | bytes 786440 | tf_op jit(solution)/shard_map/ppermute | solution.py:23
  118.7 5.5 %copy-start.12 = (bf16[3,512,128]{2,1,0:T(8,128)(2,1)}, bf16[3,512,128]{2,1,0:T(8,128)(2,1)S(1)}, u32[]{:S(2)}) copy-start(bf16[3,512,128]{2,1,0:T(8,128)(2,1)S(1)} %collective-permute-done.2.refs_2_) | copy-start | bytes 1179652
  118.7 14.5 %copy-start.9 = (bf16[4,256,128]{2,1,0:T(8,128)(2,1)S(1)}, bf16[4,256,128]{2,1,0:T(8,128)(2,1)}, u32[]{:S(2)}) copy-start(bf16[4,256,128]{2,1,0:T(8,128)(2,1)} %get-tuple-element.22) | copy-start | bytes 786436
  118.7 14.7 %copy-start.10 = (bf16[4,256,128]{2,1,0:T(8,128)(2,1)S(1)}, bf16[4,256,128]{2,1,0:T(8,128)(2,1)}, u32[]{:S(2)}) copy-start(bf16[4,256,128]{2,1,0:T(8,128)(2,1)} %get-tuple-element.24) | copy-start | bytes 786436
  118.7 14.6 %collective-permute-start.11 = (bf16[4,256,128]{2,1,0:T(8,128)(2,1)}, bf16[4,256,128]{2,1,0:T(8,128)(2,1)S(1)}, u32[]{:S(2)}, u32[]{:S(2)}) collective-permute-start(bf16[4,256,128]{2,1,0:T(8,128)(2,1)} %get-tuple-element.23), channel_id=1, source_target_pairs={{0,1},{1,0},{2,3},{3,2},{4,5},{5,4},{6,7},{7,6},{8,9},{9,8},{10,11... | collective-permute-start | bytes 786440 | tf_op jit(solution)/shard_map/ppermute | solution.py:23
  133.1 6.2 %copy-start.8 = (bf16[4,256,128]{2,1,0:T(8,128)(2,1)S(1)}, bf16[4,256,128]{2,1,0:T(8,128)(2,1)}, u32[]{:S(2)}) copy-start(bf16[4,256,128]{2,1,0:T(8,128)(2,1)} %get-tuple-element.25) | copy-start | bytes 786436
  133.1 6.2 %collective-permute-start.3 = (bf16[4,256,128]{2,1,0:T(8,128)(2,1)}, bf16[4,256,128]{2,1,0:T(8,128)(2,1)S(1)}, u32[]{:S(2)}, u32[]{:S(2)}) collective-permute-start(bf16[4,256,128]{2,1,0:T(8,128)(2,1)} %get-tuple-element.18), channel_id=1, source_target_pairs={{0,1},{1,0},{2,3},{3,2},{4,5},{5,4},{6,7},{7,6},{8,9},{9,8},{10,11... | collective-permute-start | bytes 786440 | tf_op jit(solution)/shard_map/ppermute | solution.py:23
  133.6 17.3 %collective-permute-start.14 = (bf16[256,256]{1,0:T(8,128)(2,1)S(1)}, bf16[256,256]{1,0:T(8,128)(2,1)S(1)}, u32[]{:S(2)}, u32[]{:S(2)}) collective-permute-start(bf16[256,256]{1,0:T(8,128)(2,1)S(1)} %pad_maximum_fusion.11), channel_id=1, source_target_pairs={{0,4},{4,8},{8,12},{12,0},{1,5},{5,9},{9,13},{13,1},{2,6},{6,10},{... | collective-permute-start | bytes 393224 | tf_op jit(solution)/shard_map/ppermute | solution.py:23
  134.2 15.3 %collective-permute-start.13 = (bf16[256,256]{1,0:T(8,128)(2,1)S(1)}, bf16[256,256]{1,0:T(8,128)(2,1)S(1)}, u32[]{:S(2)}, u32[]{:S(2)}) collective-permute-start(bf16[256,256]{1,0:T(8,128)(2,1)S(1)} %pad_maximum_fusion.10), channel_id=1, source_target_pairs={{0,8},{4,12},{8,0},{12,4},{1,9},{5,13},{9,1},{13,5},{2,10},{6,14},... | collective-permute-start | bytes 393224 | tf_op jit(solution)/shard_map/ppermute | solution.py:23
  136.3 19.8 %copy-start.3 = (bf16[256,1536]{1,0:T(8,128)(2,1)S(1)}, bf16[256,1536]{1,0:T(8,128)(2,1)}, u32[]{:S(2)}) copy-start(bf16[256,1536]{1,0:T(8,128)(2,1)} %get-tuple-element.27) | copy-start | bytes 2359300
  136.3 8.4 %collective-permute-start.12 = (bf16[256,256]{1,0:T(8,128)(2,1)S(1)}, bf16[256,256]{1,0:T(8,128)(2,1)S(1)}, u32[]{:S(2)}, u32[]{:S(2)}) collective-permute-start(bf16[256,256]{1,0:T(8,128)(2,1)S(1)} %pad_maximum_fusion.9), channel_id=1, source_target_pairs={{0,12},{4,0},{8,4},{12,8},{1,13},{5,1},{9,5},{13,9},{2,14},{6,2},{... | collective-permute-start | bytes 393224 | tf_op jit(solution)/shard_map/ppermute | solution.py:23
  139.4 11.5 %collective-permute-start.15 = (bf16[256,128]{1,0:T(8,128)(2,1)S(1)}, bf16[256,128]{1,0:T(8,128)(2,1)S(1)}, u32[]{:S(2)}, u32[]{:S(2)}) collective-permute-start(bf16[256,128]{1,0:T(8,128)(2,1)S(1)} %get-tuple-element.54), channel_id=1, source_target_pairs={{0,12},{4,0},{8,4},{12,8},{1,13},{5,1},{9,5},{13,9},{2,14},{6,2},{... | collective-permute-start | bytes 196616 | tf_op jit(solution)/shard_map/ppermute | solution.py:23
  144.7 7.3 %collective-permute-start.16 = (bf16[256,128]{1,0:T(8,128)(2,1)S(1)}, bf16[256,128]{1,0:T(8,128)(2,1)S(1)}, u32[]{:S(2)}, u32[]{:S(2)}) collective-permute-start(bf16[256,128]{1,0:T(8,128)(2,1)S(1)} %get-tuple-element.53), channel_id=1, source_target_pairs={{0,8},{4,12},{8,0},{12,4},{1,9},{5,13},{9,1},{13,5},{2,10},{6,14},... | collective-permute-start | bytes 196616 | tf_op jit(solution)/shard_map/ppermute | solution.py:23
  149.5 6.6 %collective-permute-start.17 = (bf16[256,128]{1,0:T(8,128)(2,1)S(1)}, bf16[256,128]{1,0:T(8,128)(2,1)S(1)}, u32[]{:S(2)}, u32[]{:S(2)}) collective-permute-start(bf16[256,128]{1,0:T(8,128)(2,1)S(1)} %get-tuple-element.52), channel_id=1, source_target_pairs={{0,4},{4,8},{8,12},{12,0},{1,5},{5,9},{9,13},{13,1},{2,6},{6,10},{... | collective-permute-start | bytes 196616 | tf_op jit(solution)/shard_map/ppermute | solution.py:23
  (5 other events, 5.9 us)
